TPU v7x, 32 devices: a whole 2x2x4 slice. The times are simulated.
32 devices in a mesh: grp: 2 (over y), gx: 4 (over z), row: 2 (over x), pb: 2 (over core).
Axes of the slice: x: 2, y: 2, z: 4, core: 2. Of those that a mesh axis runs over, the one named last changes fastest.
Arguments:
- features: bfloat16 [2048, 16, 512], P(('grp', 'gx', 'row')), parts along dimension 0, may hold values from -720 to 720
- query_pool: bfloat16 [512, 16, 512], P(None, 'gx'), may hold values from -6 to 6
- query_ids: int32 [256], P('pb'), may hold values from 0 to 511
Outputs:
- scores: float32 [2048, 256], P(('grp', 'gx', 'row'), 'pb'), parts along dimension 0
There are 2 independent parts, one for each index of `grp`. A program takes and returns all parts, laid end to end along the dimension named above; an argument that names none is the same for every part. Nothing has to cross between parts.
All inputs are finite; a program needn't handle non-finite values.
Results may differ from a plain program's by a relative error of at most 0.0035.
Values may be sent and summed in bfloat16 or wider, within the bound.
No kernel may reach another device: no remote copies, remote signals or barrier semaphores. Data moves between devices by JAX's collectives and lax.ppermute only.
A program may use at most 64 MiB of HBM per device.

v0:
```python
import jax
import jax.numpy as jnp
from jax import lax
from jax.sharding import PartitionSpec as P

ITERS = 4


def shards(features, query_pool, query_ids):
    ex_dev, modules, feat = features.shape
    regrouped = lax.all_to_all(features, "gx", split_axis=1, concat_axis=0, tiled=True)
    count = regrouped.shape[0] * lax.axis_size("row")
    grams = jnp.einsum("emk,emj->mkj", regrouped, regrouped, preferred_element_type=jnp.float32)
    grams = lax.psum(grams, "row")
    total = lax.psum(jnp.sum(jnp.trace(grams, axis1=1, axis2=2)), "gx")
    damping = 0.5 * total / (count * modules * feat)
    identity = jnp.eye(feat, dtype=jnp.float32)
    hessian = grams / count + damping * identity
    frob = jnp.sqrt(jnp.sum(hessian * hessian, axis=(1, 2)) + 1e-06)
    inverse = identity[None] / frob[:, None, None]
    for step in range(ITERS):
        product = jnp.matmul(hessian, inverse, precision=lax.Precision.HIGHEST)
        inverse = 2.0 * inverse - jnp.matmul(inverse, product, precision=lax.Precision.HIGHEST)
    picked = jnp.take(query_pool, query_ids, axis=0)
    precond = jnp.einsum(
        "qmk,mkj->qmj", picked.astype(jnp.float32), inverse, precision=lax.Precision.HIGHEST
    ).astype(jnp.bfloat16)
    local_queries = precond.shape[0]
    flat_query = precond.reshape(local_queries, -1)
    return lax.psum_scatter(
        jnp.einsum(
            "ea,qa->eq",
            regrouped.reshape(ex_dev * lax.axis_size("gx"), -1),
            flat_query,
            preferred_element_type=jnp.float32,
        ),
        "gx",
        scatter_dimension=0,
        tiled=True,
    )


def solution(mesh):
    in_specs = (P(("grp", "gx", "row"), None, None), P(None, "gx", None), P("pb"))
    out_specs = P(("grp", "gx", "row"), "pb")
    return jax.shard_map(shards, mesh=mesh, in_specs=in_specs, out_specs=out_specs, check_vma=False)
```

profile of v0, /device:TPU:0, one launch (start us, length us, event | category | flops | bytes accessed | tf_op | source)
XLA Modules:
  0.0 292.1 jit_solution(4186076273165691516)
XLA Ops:
  6.5 0.0 copy-start
  6.5 0.0 all-reduce.2.cloned.1.call-start
  6.5 2.9 copy.15
  9.4 54.3 %all_to_all.18 = bf16[128,16,512]{2,0,1:T(8,128)(2,1)S(1)} all-to-all(bf16[128,16,512]{2,0,1:T(8,128)(2,1)S(1)} %copy.15), channel_id=1, replica_groups=mesh['grp'=2,'gx'=4,'row'=2,'pb'=2] {'gx'}, dimensions={1} | all-to-all | bytes 4194304 | tf_op jit(solution)/shard_map/all_to_all | solution.py:11
  63.8 1.6 copy.29
  65.4 0.0 copy-start.2
  65.4 1.4 copy-done.2
  66.8 0.4 copy.17
  67.2 3.3 %fusion.37 = f32[4,512,512]{2,1,0:T(8,128)} fusion(bf16[512,4,512]{2,0,1:T(8,128)(2,1)S(1)} %bitcast.28), kind=kOutput, calls=%fused_computation.48 | convolution fusion | flops 1073741824 | bytes 6291456 | tf_op jit(solution)/shard_map/emk,emj->mkj/dot_general | solution.py:13
  70.5 0.0 copy-start.6
  70.5 0.0 all-reduce.2.cloned.1.call-update
  70.5 0.0 reduce-scatter.2.cloned.1.call-start
  70.6 0.6 copy-done.6
  71.2 0.0 copy-done
  71.2 1.0 gather_fusion
  72.2 0.1 iota_compare_fusion
  72.3 1.1 fusion.29
  73.4 0.3 broadcast_select_fusion
  73.7 104.0 %all-reduce.2.cloned.1.call-done = f32[4,512,512]{2,1,0:T(8,128)} async-done(((f32[4,512,512]{2,1,0:T(8,128)}), f32[4,512,512]{2,1,0:T(8,128)}) %all-reduce.2.cloned.1.call-update) | async-done | bytes 4194320 | tf_op jit(solution)/shard_map/psum | solution.py:14
  177.8 0.0 copy-start.3
  177.8 4.0 %select_reduce_fusion = f32[]{:T(128)} fusion(f32[4,512,512]{2,1,0:T(8,128)} %all-reduce.2.cloned.1.call-done, pred[512,512]{1,0:T(8,128)(4,1)S(1)} %iota_compare_fusion), kind=kLoop, calls=%fused_computation.8 | loop fusion | flops 2097151 | bytes 4456452 | tf_op jit(solution)/shard_map/reduce_sum | solution.py:15
  181.8 0.0 copy-done.3
  181.8 2.0 copy.24
  183.7 12.3 %psum.15 = f32[]{:T(128)} all-reduce(f32[]{:T(128)} %select_reduce_fusion), channel_id=1, replica_groups=mesh['grp'=2,'gx'=4,'row'=2,'pb'=2] {'gx'}, use_global_device_ids=true, to_apply=%region_2.3 | all-reduce | flops 1 | bytes 8 | tf_op jit(solution)/shard_map/psum | solution.py:15
  196.7 0.0 copy-start.1
  196.7 0.0 copy-start.5
  196.7 0.1 fusion.28
  196.8 3.1 %multiply_reduce_fusion = f32[4]{0:T(128)S(1)} fusion(f32[4,512,512]{2,1,0:T(8,128)} %all-reduce.2.cloned.1.call-done, f32[512,512]{1,0:T(8,128)S(1)} %fusion.28), kind=kLoop, calls=%fused_computation.7 | loop fusion | flops 4194300 | bytes 5242896 | tf_op jit(solution)/shard_map/reduce_sum | solution.py:19
  200.0 0.2 copy-done.1
  200.1 0.3 copy-done.5
  200.4 7.8 %fusion.5 = f32[4,512,512]{2,1,0:T(8,128)S(1)} fusion(f32[4,512,512]{2,1,0:T(8,128)S(1)} %copy-done.1, f32[4]{0:T(128)S(1)} %add_sqrt_fusion, f32[512,512]{1,0:T(8,128)S(1)} %fusion.28, f32[512,512]{1,0:T(8,128)S(1)} %copy-done.5), kind=kOutput, calls=%fused_computation.12 | convolution fusion | flops 6445596672 | bytes 10485776 | tf_op jit(solution)/shard_map/dot_general | solution.py:22
  208.2 7.8 %multiply_subtract_fusion.2 = f32[4,512,512]{2,1,0:T(8,128)S(1)} fusion(f32[4,512,512]{2,1,0:T(8,128)S(1)} %fusion.5, f32[4]{0:T(128)S(1)} %add_sqrt_fusion, f32[512,512]{1,0:T(8,128)S(1)} %copy-done.5), kind=kOutput, calls=%fused_computation.6 | convolution fusion | flops 6446645248 | bytes 9437200 | tf_op jit(solution)/shard_map/dot_general | solution.py:23
  216.0 7.4 %fusion.9 = f32[4,512,512]{2,1,0:T(8,128)S(1)} fusion(f32[4,512,512]{2,1,0:T(8,128)S(1)} %multiply_subtract_fusion.2, f32[4,512,512]{2,1,0:T(8,128)S(1)} %copy-done.1, f32[512,512]{1,0:T(8,128)S(1)} %fusion.28), kind=kOutput, calls=%fused_computation.16 | convolution fusion | flops 6444548096 | bytes 13631488 | tf_op jit(solution)/shard_map/dot_general | solution.py:22
  223.4 7.6 %multiply_subtract_fusion.1 = f32[4,512,512]{2,1,0:T(8,128)S(1)} fusion(f32[4,512,512]{2,1,0:T(8,128)S(1)} %multiply_subtract_fusion.2, f32[4,512,512]{2,1,0:T(8,128)S(1)} %fusion.9), kind=kOutput, calls=%fused_computation.5 | convolution fusion | flops 6444548096 | bytes 12582912 | tf_op jit(solution)/shard_map/dot_general | solution.py:23
  231.1 7.4 %fusion.8 = f32[4,512,512]{2,1,0:T(8,128)S(1)} fusion(f32[4,512,512]{2,1,0:T(8,128)S(1)} %multiply_subtract_fusion.1, f32[4,512,512]{2,1,0:T(8,128)S(1)} %copy-done.1, f32[512,512]{1,0:T(8,128)S(1)} %fusion.28), kind=kOutput, calls=%fused_computation.15 | convolution fusion | flops 6444548096 | bytes 13631488 | tf_op jit(solution)/shard_map/dot_general | solution.py:22
  238.4 7.7 %multiply_subtract_fusion = f32[4,512,512]{2,1,0:T(8,128)S(1)} fusion(f32[4,512,512]{2,1,0:T(8,128)S(1)} %multiply_subtract_fusion.1, f32[4,512,512]{2,1,0:T(8,128)S(1)} %fusion.8), kind=kOutput, calls=%fused_computation.4 | convolution fusion | flops 6444548096 | bytes 12582912 | tf_op jit(solution)/shard_map/dot_general | solution.py:23
  246.1 7.4 %fusion.7 = f32[4,512,512]{2,1,0:T(8,128)S(1)} fusion(f32[4,512,512]{2,1,0:T(8,128)S(1)} %multiply_subtract_fusion, f32[4,512,512]{2,1,0:T(8,128)S(1)} %copy-done.1, f32[512,512]{1,0:T(8,128)S(1)} %fusion.28), kind=kOutput, calls=%fused_computation.14 | convolution fusion | flops 6444548096 | bytes 13631488 | tf_op jit(solution)/shard_map/dot_general | solution.py:22
  253.5 7.6 %fusion.38 = f32[4,512,512]{2,1,0:T(8,128)S(1)} fusion(f32[4,512,512]{2,1,0:T(8,128)S(1)} %multiply_subtract_fusion, f32[4,512,512]{2,1,0:T(8,128)S(1)} %fusion.7), kind=kOutput, calls=%fused_computation.49 | convolution fusion | flops 6442450944 | bytes 12582912 | tf_op jit(solution)/shard_map/dot_general | solution.py:23
  261.1 0.0 copy-start.4
  261.1 3.6 %fusion.25 = bf16[4,512,128]{2,1,0:T(8,128)(2,1)S(1)} fusion(f32[4,512,512]{2,1,0:T(8,128)S(1)} %fusion.38, f32[4,512,512]{2,1,0:T(8,128)S(1)} %multiply_subtract_fusion, bf16[128,4,512]{2,1,0:T(4,128)(2,1)S(1)} %broadcast_select_fusion), kind=kOutput, calls=%fused_computation.30 | convolution fusion | flops 1612972032 | bytes 9437184 | tf_op jit(solution)/shard_map/qmk,mkj->qmj/dot_general | solution.py:25
  264.7 0.0 copy-done.4
  264.7 1.5 convolution_bitcast_fusion
  266.2 0.0 reduce-scatter.2.cloned.1.call-update
  266.3 17.0 %reduce-scatter.2.cloned.1.call-done = f32[128,128]{0,1:T(8,128)} async-done(((f32[512,128]{0,1:T(8,128)}), f32[128,128]{0,1:T(8,128)}) %reduce-scatter.2.cloned.1.call-update) | async-done | bytes 65552 | tf_op jit(solution)/shard_map/reduce_scatter | solution.py:30
  283.3 1.6 copy.21
  (4 shorter events, 0.0 us)
Async XLA Ops:
  6.5 64.6 %copy-start = (bf16[512,4,512]{2,1,0:T(4,128)(2,1)S(1)}, bf16[512,4,512]{2,1,0:T(4,128)(2,1)}, u32[]{:S(2)}) copy-start(bf16[512,4,512]{2,1,0:T(4,128)(2,1)} %param.4) | copy-start | bytes 6291460
  6.5 171.2 %all-reduce.2.cloned.1.call-start = ((), (), s32[]{:S(2)}) async-start(), calls=%async_computation.2 | async-start | bytes 8388608 | tf_op jit(solution)/shard_map/psum | solution.py:14
  65.4 1.4 copy-start.2
  70.5 0.7 copy-start.6
  70.5 212.8 %reduce-scatter.2.cloned.1.call-start = ((), (), s32[]{:S(2)}) async-start(), calls=%async_computation.3 | async-start | bytes 327680 | tf_op jit(solution)/shard_map/reduce_scatter | solution.py:30
  177.8 4.0 %copy-start.3 = (bf16[128,4,4,512]{3,2,0,1:T(4,128)(2,1)S(1)}, bf16[128,4,4,512]{3,2,0,1:T(4,128)(2,1)}, u32[]{:S(2)}) copy-start(bf16[128,4,4,512]{3,2,0,1:T(4,128)(2,1)} %copy-done.2) | copy-start | bytes 6291460
  196.7 3.5 %copy-start.1 = (f32[4,512,512]{2,1,0:T(8,128)S(1)}, f32[4,512,512]{2,1,0:T(8,128)}, u32[]{:S(2)}) copy-start(f32[4,512,512]{2,1,0:T(8,128)} %all-reduce.2.cloned.1.call-done) | copy-start | bytes 12582916
  196.7 3.7 %copy-start.5 = (f32[512,512]{1,0:T(8,128)S(1)}, f32[512,512]{1,0:T(8,128)}, u32[]{:S(2)}) copy-start(f32[512,512]{1,0:T(8,128)} %fusion.29) | copy-start | bytes 3145732
  261.1 3.6 %copy-start.4 = (bf16[64,8,4,512]{3,1,2,0:T(8,128)(2,1)S(1)}, bf16[64,8,4,512]{3,1,2,0:T(8,128)(2,1)}, u32[]{:S(2)}) copy-start(bf16[64,8,4,512]{3,1,2,0:T(8,128)(2,1)} %copy.24) | copy-start | bytes 6291460
Sparse Core Ops, SparseCore 0:
  70.6 107.0 all-reduce.1
  266.4 16.8 reduce-scatter.1
where the time goes:
time: 298 us; the launch traced here: 292 us
  waiting for transfers between devices  121 us (41%)
  matrix products  69 us (23%)
  blocking collectives  66.6 us (22%)
  between operations  14.7 us (5%)
  local copies, waits for them, and re-layouts  12 us (4%)
  other arithmetic  8.8 us (3%)
    psum x1, waiting for transfers between devices, shards(): grams = lax.psum(grams, 'row')  104 us
    all_to_all x1, blocking collectives, shards(): lax.all_to_all(features, 'gx', split_axis=1, concat_axis=0, tiled=True)  54.3 us
    dot_general x4, matrix products, shards(): jnp.matmul(inverse, product, precision=lax.Precision.HIGHEST)  30.7 us
    dot_general x4, matrix products, shards(): product = jnp.matmul(hessian, inverse, precision=lax.Precision.HIGHEST)  29.9 us
    reduce_scatter x1, waiting for transfers between devices, shards(): lax.psum_scatter(jnp.einsum('ea,qa->eq', regrouped.reshape(ex_dev * lax.a...  17 us
    psum x1, blocking collectives, shards(): total = lax.psum(jnp.sum(jnp.trace(grams, axis1=1, axis2=2)), 'gx')  12.3 us
    unnamed x16, local copies, waits for them, and re-layouts  7.31 us
  transfers between devices with their start and end apart: 2, of which 2 were waited for; matrix products, arithmetic and copies ran while one was open for 1% of the time, Pallas kernels for 0%

commit v1 on v0

--- a/solution.py
+++ b/solution.py
@@ -1,12 +1,175 @@
+import functools
+
 import jax
 import jax.numpy as jnp
 from jax import lax
+from jax.experimental import pallas as pl
+from jax.experimental.pallas import tpu as pltpu
 from jax.sharding import PartitionSpec as P
 
 ITERS = 4
-
-
-def shards(features, query_pool, query_ids):
+BF16 = jnp.bfloat16
+F32 = jnp.float32
+LANES = 128
+GROUP = ("gx", "row")
+VMEM = pl.BlockSpec(memory_space=pltpu.VMEM)
+
+
+def dot(a, b, dims):
+    return lax.dot_general(a, b, (dims, ((), ())), preferred_element_type=F32)
+
+
+def split(a):
+    high = a.astype(BF16)
+    return high, (a - high.astype(F32)).astype(BF16)
+
+
+def pack_kernel(peers, feats, *outs):
+    ex_dev, modules, feat = feats.shape
+    cols = feat // LANES
+    step = 256 // modules
+    me = lax.axis_index("gx") * lax.axis_size("row") + lax.axis_index("row")
+    side = lax.axis_index("pb")
+    r = lax.broadcasted_iota(jnp.int32, (peers * step, step * modules), 0)
+    c = lax.broadcasted_iota(jnp.int32, (peers * step, step * modules), 1)
+    wanted = ((r // step) ^ me) * lax.axis_size("pb") + side
+    pick = ((c // modules == r % step) & (c % modules == wanted)).astype(F32).astype(BF16)
+
+    def body(b, acc):
+        x = feats[pl.ds(b * step, step)].reshape(step * modules, feat)
+        y = dot(pick, x, ((1,), (0,))).astype(BF16)
+        for k in range(peers):
+            for j in range(cols):
+                start = pl.multiple_of(j * ex_dev + b * step, step)
+                outs[k][pl.ds(start, step), :] = y[k * step : (k + 1) * step, j * LANES : (j + 1) * LANES]
+        xf = x.astype(F32)
+        sq = xf * xf
+        return acc + sq.reshape(step * modules // 8, 8, feat).sum(0)
+
+    acc = lax.fori_loop(0, ex_dev // step, body, jnp.zeros((8, feat), F32))
+    lane = acc.sum(0, keepdims=True)
+    lane = sum(lane[:, j * LANES : (j + 1) * LANES] for j in range(cols))
+    high, rest = split(lane)
+    mid, low = split(lane - high.astype(F32))
+    row = lax.broadcasted_iota(jnp.int32, (8, LANES), 0)
+    high, mid, low = (jnp.broadcast_to(v.astype(F32), (8, LANES)) for v in (high, mid, low))
+    tail = jnp.where(row == 0, high, jnp.where(row == 1, mid, jnp.where(row == 2, low, 0.0)))
+    for k in range(peers):
+        outs[k][pl.ds(cols * ex_dev, 8), :] = tail.astype(BF16)
+
+
+def pack(features, peers):
+    ex_dev, modules, feat = features.shape
+    shape = jax.ShapeDtypeStruct((feat // LANES * ex_dev + 8, LANES), BF16)
+    return pl.pallas_call(
+        functools.partial(pack_kernel, peers),
+        out_shape=[shape] * peers,
+        in_specs=[VMEM],
+        out_specs=[VMEM] * peers,
+        name="pack",
+    )(features)
+
+
+def pick_kernel(pool, ids, out):
+    rows, queries = pool.shape[0] * pool.shape[1], ids.shape[1]
+    local = lax.axis_index("row") * lax.axis_size("pb") + lax.axis_index("pb")
+    wanted = ids[...] * pool.shape[1] + local
+    r = lax.broadcasted_iota(jnp.int32, (rows, queries), 0)
+    chosen = (r == wanted).astype(F32).astype(BF16)
+    flat = pool[...].reshape(rows, pool.shape[2])
+    out[...] = dot(chosen, flat, ((0,), (0,))).astype(BF16)
+
+
+def pick(query_pool, ids):
+    return pl.pallas_call(
+        pick_kernel,
+        out_shape=jax.ShapeDtypeStruct((ids.shape[1], query_pool.shape[2]), BF16),
+        in_specs=[VMEM, VMEM],
+        out_specs=VMEM,
+        name="pick",
+    )(query_pool, ids)
+
+
+def score_kernel(modules, *refs):
+    peers = len(refs) - 4
+    chunks, (picked, own, other, feats) = refs[:peers], refs[peers:]
+    count, feat = feats.shape
+    ex_dev = count // peers
+    cols = feat // LANES
+    total = jnp.zeros((1, LANES), F32)
+    for k in range(peers):
+        for j in range(cols):
+            feats[k * ex_dev : (k + 1) * ex_dev, j * LANES : (j + 1) * LANES] = chunks[k][j * ex_dev : (j + 1) * ex_dev, :]
+        total = total + chunks[k][cols * ex_dev :, :].astype(F32).sum(0, keepdims=True)
+    total = jnp.sum(total)
+    damping = 0.5 * total / (count * modules * feat)
+    f = feats[...]
+    gram = dot(f, f, ((0,), (0,)))
+    diag = lax.broadcasted_iota(jnp.int32, (feat, feat), 0) == lax.broadcasted_iota(jnp.int32, (feat, feat), 1)
+    hessian = gram / count + jnp.where(diag, damping, 0.0)
+    inv = 1.0 / jnp.sqrt(jnp.sum(hessian * hessian) + 1e-06)
+    plain = ((1,), (0,))
+
+    def apply(v, mat):
+        vh, vl = split(v)
+        mh, ml = mat
+        return dot(vh, mh, plain) + (dot(vl, mh, plain) + dot(vh, ml, plain))
+
+    b1 = hessian * inv
+    m1 = split(b1)
+    b2 = 2.0 * b1 - dot(m1[0], m1[0], plain)
+    m2 = split(b2)
+    b4 = 2.0 * b2 - dot(m2[0], m2[0], plain)
+    m4 = split(b4)
+    v = picked[...]
+    v = 2.0 * v.astype(F32) - (dot(v, m1[0], plain) + dot(v, m1[1], plain))
+    v = 2.0 * v - apply(v, m2)
+    v = 2.0 * v - apply(v, m4)
+    w = v - apply(v, m4)
+    w = w - apply(w, m4)
+    precond = ((v + w) * inv).astype(BF16)
+    half = precond.shape[0] // 2
+    other[...] = dot(f, precond[half:], ((1,), (1,)))
+    own[...] = dot(f, precond[:half], ((1,), (1,)))
+
+
+def score(chunks, picked, modules):
+    peers = len(chunks)
+    queries, feat = picked.shape
+    count = peers * (chunks[0].shape[0] - 8) * LANES // feat
+    half = jax.ShapeDtypeStruct((count, queries // 2), F32)
+    return pl.pallas_call(
+        functools.partial(score_kernel, modules),
+        out_shape=[half, half],
+        in_specs=[VMEM] * (peers + 1),
+        out_specs=[VMEM, VMEM],
+        scratch_shapes=[pltpu.VMEM((count, feat), BF16)],
+        name="score",
+    )(*chunks, picked)
+
+
+def exchange(x, axes, k, size):
+    return lax.ppermute(x, axes, [(i, i ^ k) for i in range(size)])
+
+
+def owned(features, query_pool, query_ids):
+    ex_dev, modules, feat = features.shape
+    peers = lax.axis_size("gx") * lax.axis_size("row")
+    ids = jnp.concatenate([query_ids, exchange(query_ids, "pb", 1, 2)])[None, :]
+    chunks = list(pack(features, peers))
+    for k in (6, 7, 4, 5, 2, 3, 1):
+        chunks[k] = exchange(chunks[k], GROUP, k, peers)
+    picked = pick(query_pool, ids)
+    own, other = score(chunks, picked, modules)
+    part = own + exchange(other, "pb", 1, 2)
+    part = part.reshape(2, 4, ex_dev, -1)
+    near = part[:, 0]
+    for k in (1, 2, 3):
+        near = near + exchange(part[:, k].astype(BF16), GROUP, k, peers).astype(F32)
+    return near[0] + exchange(near[1].astype(BF16), GROUP, 4, peers).astype(F32)
+
+
+def regrouped(features, query_pool, query_ids):
     ex_dev, modules, feat = features.shape
     regrouped = lax.all_to_all(features, "gx", split_axis=1, concat_axis=0, tiled=True)
     count = regrouped.shape[0] * lax.axis_size("row")
@@ -40,6 +203,14 @@
     )
 
 
+def shards(features, query_pool, query_ids):
+    modules = features.shape[1]
+    gx, row, pb = (lax.axis_size(name) for name in ("gx", "row", "pb"))
+    if (gx, row, pb) == (4, 2, 2) and modules == gx * row * pb:
+        return owned(features, query_pool, query_ids)
+    return regrouped(features, query_pool, query_ids)
+
+
 def solution(mesh):
     in_specs = (P(("grp", "gx", "row"), None, None), P(None, "gx", None), P("pb"))
     out_specs = P(("grp", "gx", "row"), "pb")

time: 298 us -> 60.4 us (0.20); the launches traced: 292 us -> 60.2 us
  waiting for transfers between devices: 121 us -> 19.2 us
  matrix products: 69 us -> 0 us
  blocking collectives: 66.6 us -> 0 us
  starting transfers between devices: 0.04 us -> 23.2 us
  between operations: 14.7 us -> 0.09 us
  Pallas kernels: 0 us -> 14.5 us
  local copies, waits for them, and re-layouts: 12 us -> 0.75 us
  other arithmetic: 8.8 us -> 2.35 us
    psum x1 -> x0, waiting for transfers between devices: 104 us -> none  [shards(): grams = lax.psum(grams, 'row')]
    dot_general x11 -> x0, matrix products: 69 us -> none  [the longest x4 30.7 us: shards(): jnp.matmul(inverse, product, precision=lax.Precision.HIGHEST)]
    all_to_all x1 -> x0, blocking collectives: 54.3 us -> none  [shards(): lax.all_to_all(features, 'gx', split_axis=1, concat_axis=0, tiled=True)]
    ppermute x0 -> x13, starting transfers between devices: none -> 23.2 us  [exchange(): return lax.ppermute(x, axes, [(i, i ^ k) for i in range(size)])]
    ppermute x0 -> x13, waiting for transfers between devices: none -> 19.2 us  [exchange(): return lax.ppermute(x, axes, [(i, i ^ k) for i in range(size)])]
    reduce_scatter x1 -> x0, waiting for transfers between devices: 17 us -> none  [shards(): lax.psum_scatter(jnp.einsum('ea,qa->eq', regrouped.reshape(ex_dev * lax.a...]
    pallas_call x0 -> x3, Pallas kernels: none -> 14.5 us  [the longest x1 7.27 us: score(): pl.pallas_call(functools.partial(score_kernel, modules), out_shape=[half,...]
    psum x1 -> x0, blocking collectives: 12.3 us -> none  [shards(): total = lax.psum(jnp.sum(jnp.trace(grams, axis1=1, axis2=2)), 'gx')]
  transfers between devices with their start and end apart: 2 -> 13, of which waited for: 2 -> 5; matrix products, arithmetic and copies ran while one was open for 1% -> 1% of each run, Pallas kernels for 0% -> 5%
where the time goes in v1:
time: 60.4 us; the launch traced here: 60.2 us
  starting transfers between devices  23.2 us (38%)
  waiting for transfers between devices  19.2 us (32%)
  Pallas kernels  14.5 us (24%)
  other arithmetic  2.35 us (4%)
  local copies, waits for them, and re-layouts  0.75 us (1%)
    ppermute x13, starting transfers between devices, exchange(): return lax.ppermute(x, axes, [(i, i ^ k) for i in range(size)])  23.2 us
    ppermute x13, waiting for transfers between devices, exchange(): return lax.ppermute(x, axes, [(i, i ^ k) for i in range(size)])  19.2 us
    pallas_call x1, Pallas kernels, score(): pl.pallas_call(functools.partial(score_kernel, modules), out_shape=[half,...  7.27 us
    pallas_call x1, Pallas kernels, pack(): pl.pallas_call(functools.partial(pack_kernel, peers), out_shape=[shape] *...  4.2 us
    pallas_call x1, Pallas kernels, pick(): pl.pallas_call(pick_kernel, out_shape=jax.ShapeDtypeStruct((ids.shape[1],...  3.04 us
  transfers between devices with their start and end apart: 13, of which 5 were waited for; matrix products, arithmetic and copies ran while one was open for 1% of the time, Pallas kernels for 5%

profile of v1, /device:TPU:0, one launch (start us, length us, event | category | flops | bytes accessed | tf_op | source)
XLA Modules:
  0.0 60.2 jit_solution(7449871441672863706)
XLA Ops:
  0.0 0.0 copy-start.7
  0.0 4.2 %pack.1 = (bf16[520,128]{1,0:T(8,128)(2,1)}, bf16[520,128]{1,0:T(8,128)(2,1)}, bf16[520,128]{1,0:T(8,128)(2,1)}, bf16[520,128]{1,0:T(8,128)(2,1)}, bf16[520,128]...) custom-call(bf16[128,16,512]{2,1,0:T(8,128)(2,1)} %feats.1), custom_call_target="tpu_custom_call" | custom-call | tf_op jit(solution)/shard_map/pack/pallas_call | solution.py:64
  4.2 2.9 %collective-permute-start = (bf16[520,128]{1,0:T(8,128)(2,1)}, bf16[520,128]{1,0:T(8,128)(2,1)S(1)}, u32[]{:S(2)}, u32[]{:S(2)}) collective-permute-start(bf16[520,128]{1,0:T(8,128)(2,1)} %get-tuple-element.16), channel_id=1, source_target_pairs={{0,2},{2,0},{4,6},{6,4},{8,10},{10,8},{12,14},{14,12},{1,3},{3,1},... | collective-permute-start | bytes 399368 | tf_op jit(solution)/shard_map/ppermute | solution.py:152
  7.1 1.6 %collective-permute-start.1 = (bf16[520,128]{1,0:T(8,128)(2,1)}, bf16[520,128]{1,0:T(8,128)(2,1)S(1)}, u32[]{:S(2)}, u32[]{:S(2)}) collective-permute-start(bf16[520,128]{1,0:T(8,128)(2,1)} %get-tuple-element.17), channel_id=1, source_target_pairs={{0,4},{2,6},{4,0},{6,2},{8,12},{10,14},{12,8},{14,10},{1,5},{3,7},... | collective-permute-start | bytes 399368 | tf_op jit(solution)/shard_map/ppermute | solution.py:152
  8.7 0.0 copy-done.7
  8.7 0.0 collective-permute-start.7
  8.7 0.0 collective-permute-start.2
  8.8 3.0 %collective-permute-start.3 = (bf16[520,128]{1,0:T(8,128)(2,1)}, bf16[520,128]{1,0:T(8,128)(2,1)S(1)}, u32[]{:S(2)}, u32[]{:S(2)}) collective-permute-start(bf16[520,128]{1,0:T(8,128)(2,1)} %get-tuple-element.19), channel_id=1, source_target_pairs={{0,8},{2,10},{4,12},{6,14},{8,0},{10,2},{12,4},{14,6},{1,9},{3,11}... | collective-permute-start | bytes 399368 | tf_op jit(solution)/shard_map/ppermute | solution.py:152
  11.7 0.0 collective-permute-done.7
  11.7 1.3 %collective-permute-start.4 = (bf16[520,128]{1,0:T(8,128)(2,1)}, bf16[520,128]{1,0:T(8,128)(2,1)S(1)}, u32[]{:S(2)}, u32[]{:S(2)}) collective-permute-start(bf16[520,128]{1,0:T(8,128)(2,1)} %get-tuple-element.20), channel_id=1, source_target_pairs={{0,10},{2,8},{4,14},{6,12},{8,2},{10,0},{12,6},{14,4},{1,11},{3,9}... | collective-permute-start | bytes 399368 | tf_op jit(solution)/shard_map/ppermute | solution.py:152
  13.0 0.0 collective-permute-done.refs_1_
  13.0 0.0 copy-start
  13.0 3.6 %collective-permute-start.5 = (bf16[520,128]{1,0:T(8,128)(2,1)}, bf16[520,128]{1,0:T(8,128)(2,1)S(1)}, u32[]{:S(2)}, u32[]{:S(2)}) collective-permute-start(bf16[520,128]{1,0:T(8,128)(2,1)} %get-tuple-element.21), channel_id=1, source_target_pairs={{0,12},{2,14},{4,8},{6,10},{8,4},{10,6},{12,0},{14,2},{1,13},{3,15... | collective-permute-start | bytes 399368 | tf_op jit(solution)/shard_map/ppermute | solution.py:152
  16.6 0.0 collective-permute-done.1.refs_2_
  16.6 0.0 copy-start.1
  16.6 0.6 collective-permute-start.6
  17.2 0.6 pad_add_fusion
  17.7 3.0 %pick.1.refs_8_ = bf16[256,512]{1,0:T(8,128)(2,1)} custom-call(bf16[512,4,512]{2,1,0:T(4,128)(2,1)} %pool.1, s32[1,256]{1,0:T(1,128)} %bitcast.24), custom_call_target="tpu_custom_call" | custom-call | tf_op jit(solution)/shard_map/pick/pallas_call | solution.py:84
  20.8 0.0 collective-permute-done.2.refs_3_
  20.8 0.0 copy-start.2
  20.8 0.0 collective-permute-done.3.refs_4_
  20.8 0.0 copy-start.3
  20.8 10.9 %collective-permute-done.4.refs_5_ = bf16[520,128]{1,0:T(8,128)(2,1)S(1)} collective-permute-done((bf16[520,128]{1,0:T(8,128)(2,1)}, bf16[520,128]{1,0:T(8,128)(2,1)S(1)}, u32[]{:S(2)}, u32[]{:S(2)}) %collective-permute-start.4) | collective-permute-done | bytes 133152 | tf_op jit(solution)/shard_map/ppermute | solution.py:152
  31.7 0.0 copy-start.4
  31.7 0.0 collective-permute-done.5.refs_6_
  31.7 0.0 copy-start.5
  31.7 0.0 collective-permute-done.6.refs_7_
  31.7 0.0 copy-start.6
  31.7 0.0 copy-done
  31.7 0.0 copy-done.1
  31.8 0.0 copy-done.2
  31.8 0.0 copy-done.3
  31.8 0.6 copy-done.4
  32.4 0.0 copy-done.5
  32.4 0.1 copy-done.6
  32.5 7.3 %score.1 = (f32[1024,128]{1,0:T(8,128)}, f32[1024,128]{1,0:T(8,128)}) custom-call(bf16[520,128]{1,0:T(8,128)(2,1)} %get-tuple-element.15.refs_0_, bf16[520,128]{1,0:T(8,128)(2,1)} %copy-done, bf16[520,128]{1,0:T(8,128)(2,1)} %copy-done.1, bf16[520,128]{1,0:T(8,128)(2,1)} %copy-done.2, bf16[520,128]{1,0:T(8,128)(2,1)} %copy-done.3, ...), custom_call_target="tpu_custom_call" | custom-call | tf_op jit(solution)/shard_map/score/pallas_call | solution.py:141
  39.7 0.0 collective-permute-start.8
  39.7 2.1 %collective-permute-done.8 = f32[1024,128]{1,0:T(8,128)S(1)} collective-permute-done((f32[1024,128]{1,0:T(8,128)}, f32[1024,128]{1,0:T(8,128)S(1)}, u32[]{:S(2)}, u32[]{:S(2)}) %collective-permute-start.8) | collective-permute-done | bytes 524320 | tf_op jit(solution)/shard_map/ppermute | solution.py:152
  41.9 1.1 %add.15 = f32[1024,128]{1,0:T(8,128)S(1)} add(f32[1024,128]{1,0:T(8,128)} %get-tuple-element.23, f32[1024,128]{1,0:T(8,128)S(1)} %collective-permute-done.8) | non-fusion elementwise | flops 131072 | bytes 1572864 | tf_op jit(solution)/shard_map/add | solution.py:164
  43.0 1.2 %collective-permute-start.9 = (bf16[2,128,128]{2,1,0:T(8,128)(2,1)S(1)}, bf16[2,128,128]{2,1,0:T(8,128)(2,1)S(1)}, u32[]{:S(2)}, u32[]{:S(2)}) collective-permute-start(bf16[2,128,128]{2,1,0:T(8,128)(2,1)S(1)} %get-tuple-element.25), channel_id=1, source_target_pairs={{0,2},{2,0},{4,6},{6,4},{8,10},{10,8},{12,14},{14,12},{1,3},{3,1},... | collective-permute-start | bytes 196616 | tf_op jit(solution)/shard_map/ppermute | solution.py:152
  44.2 6.0 %collective-permute-start.11 = (bf16[2,128,128]{2,1,0:T(8,128)(2,1)S(1)}, bf16[2,128,128]{2,1,0:T(8,128)(2,1)S(1)}, u32[]{:S(2)}, u32[]{:S(2)}) collective-permute-start(bf16[2,128,128]{2,1,0:T(8,128)(2,1)S(1)} %get-tuple-element.26), channel_id=1, source_target_pairs={{0,6},{2,4},{4,2},{6,0},{8,14},{10,12},{12,10},{14,8},{1,7},{3,5},... | collective-permute-start | bytes 196616 | tf_op jit(solution)/shard_map/ppermute | solution.py:152
  50.2 0.0 collective-permute-start.10
  50.2 0.0 collective-permute-done.9
  50.2 2.2 %collective-permute-done.11 = bf16[2,128,128]{2,1,0:T(8,128)(2,1)S(1)} collective-permute-done((bf16[2,128,128]{2,1,0:T(8,128)(2,1)S(1)}, bf16[2,128,128]{2,1,0:T(8,128)(2,1)S(1)}, u32[]{:S(2)}, u32[]{:S(2)}) %collective-permute-start.11) | collective-permute-done | bytes 65568 | tf_op jit(solution)/shard_map/ppermute | solution.py:152
  52.4 2.0 %collective-permute-done.10 = bf16[2,128,128]{2,1,0:T(8,128)(2,1)S(1)} collective-permute-done((bf16[2,128,128]{2,1,0:T(8,128)(2,1)S(1)}, bf16[2,128,128]{2,1,0:T(8,128)(2,1)S(1)}, u32[]{:S(2)}, u32[]{:S(2)}) %collective-permute-start.10) | collective-permute-done | bytes 65568 | tf_op jit(solution)/shard_map/ppermute | solution.py:152
  54.5 3.2 %collective-permute-start.12 = (bf16[128,128]{1,0:T(8,128)(2,1)S(1)}, bf16[128,128]{1,0:T(8,128)(2,1)S(1)}, u32[]{:S(2)}, u32[]{:S(2)}) collective-permute-start(bf16[128,128]{1,0:T(8,128)(2,1)S(1)} %fusion.4), channel_id=1, source_target_pairs={{0,8},{2,10},{4,12},{6,14},{8,0},{10,2},{12,4},{14,6},{1,9},{3,11}... | collective-permute-start | bytes 98312 | tf_op jit(solution)/shard_map/ppermute | solution.py:152
  57.6 1.9 %collective-permute-done.12 = bf16[128,128]{1,0:T(8,128)(2,1)S(1)} collective-permute-done((bf16[128,128]{1,0:T(8,128)(2,1)S(1)}, bf16[128,128]{1,0:T(8,128)(2,1)S(1)}, u32[]{:S(2)}, u32[]{:S(2)}) %collective-permute-start.12) | collective-permute-done | bytes 32800 | tf_op jit(solution)/shard_map/ppermute | solution.py:152
  59.5 0.6 %fusion.3 = f32[128,128]{1,0:T(8,128)} fusion(f32[2,128,128]{2,1,0:T(8,128)S(1)} %fusion.2, bf16[128,128]{1,0:T(8,128)(2,1)S(1)} %collective-permute-done.12), kind=kLoop, calls=%fused_computation.6 | loop fusion | flops 32768 | bytes 163840 | tf_op jit(solution)/shard_map/add | solution.py:169
  (3 shorter events, 0.1 us)
Async XLA Ops:
  0.0 8.7 %copy-start.7 = (s32[128]{0:T(128)S(1)}, s32[128]{0:T(128)}, u32[]{:S(2)}) copy-start(s32[128]{0:T(128)} %param.5) | copy-start | bytes 1540
  4.2 8.8 %collective-permute-start = (bf16[520,128]{1,0:T(8,128)(2,1)}, bf16[520,128]{1,0:T(8,128)(2,1)S(1)}, u32[]{:S(2)}, u32[]{:S(2)}) collective-permute-start(bf16[520,128]{1,0:T(8,128)(2,1)} %get-tuple-element.16), channel_id=1, source_target_pairs={{0,2},{2,0},{4,6},{6,4},{8,10},{10,8},{12,14},{14,12},{1,3},{3,1},... | collective-permute-start | bytes 399368 | tf_op jit(solution)/shard_map/ppermute | solution.py:152
  7.1 9.5 %collective-permute-start.1 = (bf16[520,128]{1,0:T(8,128)(2,1)}, bf16[520,128]{1,0:T(8,128)(2,1)S(1)}, u32[]{:S(2)}, u32[]{:S(2)}) collective-permute-start(bf16[520,128]{1,0:T(8,128)(2,1)} %get-tuple-element.17), channel_id=1, source_target_pairs={{0,4},{2,6},{4,0},{6,2},{8,12},{10,14},{12,8},{14,10},{1,5},{3,7},... | collective-permute-start | bytes 399368 | tf_op jit(solution)/shard_map/ppermute | solution.py:152
  8.7 3.0 %collective-permute-start.7 = (s32[128]{0:T(128)S(1)}, s32[128]{0:T(128)S(1)}, u32[]{:S(2)}, u32[]{:S(2)}) collective-permute-start(s32[128]{0:T(128)S(1)} %copy-done.7), channel_id=1, source_target_pairs={{0,1},{1,0},{2,3},{3,2},{4,5},{5,4},{6,7},{7,6},{8,9},{9,8},{10,11... | collective-permute-start | bytes 1544 | tf_op jit(solution)/shard_map/ppermute | solution.py:152
  8.7 12.1 %collective-permute-start.2 = (bf16[520,128]{1,0:T(8,128)(2,1)}, bf16[520,128]{1,0:T(8,128)(2,1)S(1)}, u32[]{:S(2)}, u32[]{:S(2)}) collective-permute-start(bf16[520,128]{1,0:T(8,128)(2,1)} %get-tuple-element.18), channel_id=1, source_target_pairs={{0,6},{2,4},{4,2},{6,0},{8,14},{10,12},{12,10},{14,8},{1,7},{3,5},... | collective-permute-start | bytes 399368 | tf_op jit(solution)/shard_map/ppermute | solution.py:152
  8.8 12.0 %collective-permute-start.3 = (bf16[520,128]{1,0:T(8,128)(2,1)}, bf16[520,128]{1,0:T(8,128)(2,1)S(1)}, u32[]{:S(2)}, u32[]{:S(2)}) collective-permute-start(bf16[520,128]{1,0:T(8,128)(2,1)} %get-tuple-element.19), channel_id=1, source_target_pairs={{0,8},{2,10},{4,12},{6,14},{8,0},{10,2},{12,4},{14,6},{1,9},{3,11}... | collective-permute-start | bytes 399368 | tf_op jit(solution)/shard_map/ppermute | solution.py:152
  11.7 20.0 %collective-permute-start.4 = (bf16[520,128]{1,0:T(8,128)(2,1)}, bf16[520,128]{1,0:T(8,128)(2,1)S(1)}, u32[]{:S(2)}, u32[]{:S(2)}) collective-permute-start(bf16[520,128]{1,0:T(8,128)(2,1)} %get-tuple-element.20), channel_id=1, source_target_pairs={{0,10},{2,8},{4,14},{6,12},{8,2},{10,0},{12,6},{14,4},{1,11},{3,9}... | collective-permute-start | bytes 399368 | tf_op jit(solution)/shard_map/ppermute | solution.py:152
  13.0 18.7 %copy-start = (bf16[520,128]{1,0:T(8,128)(2,1)}, bf16[520,128]{1,0:T(8,128)(2,1)S(1)}, u32[]{:S(2)}) copy-start(bf16[520,128]{1,0:T(8,128)(2,1)S(1)} %collective-permute-done.refs_1_) | copy-start | bytes 399364
  13.0 18.7 %collective-permute-start.5 = (bf16[520,128]{1,0:T(8,128)(2,1)}, bf16[520,128]{1,0:T(8,128)(2,1)S(1)}, u32[]{:S(2)}, u32[]{:S(2)}) collective-permute-start(bf16[520,128]{1,0:T(8,128)(2,1)} %get-tuple-element.21), channel_id=1, source_target_pairs={{0,12},{2,14},{4,8},{6,10},{8,4},{10,6},{12,0},{14,2},{1,13},{3,15... | collective-permute-start | bytes 399368 | tf_op jit(solution)/shard_map/ppermute | solution.py:152
  16.6 15.1 %copy-start.1 = (bf16[520,128]{1,0:T(8,128)(2,1)}, bf16[520,128]{1,0:T(8,128)(2,1)S(1)}, u32[]{:S(2)}) copy-start(bf16[520,128]{1,0:T(8,128)(2,1)S(1)} %collective-permute-done.1.refs_2_) | copy-start | bytes 399364
  16.6 15.1 %collective-permute-start.6 = (bf16[520,128]{1,0:T(8,128)(2,1)}, bf16[520,128]{1,0:T(8,128)(2,1)S(1)}, u32[]{:S(2)}, u32[]{:S(2)}) collective-permute-start(bf16[520,128]{1,0:T(8,128)(2,1)} %get-tuple-element.22), channel_id=1, source_target_pairs={{0,14},{2,12},{4,10},{6,8},{8,6},{10,4},{12,2},{14,0},{1,15},{3,13... | collective-permute-start | bytes 399368 | tf_op jit(solution)/shard_map/ppermute | solution.py:152
  20.8 11.0 %copy-start.2 = (bf16[520,128]{1,0:T(8,128)(2,1)}, bf16[520,128]{1,0:T(8,128)(2,1)S(1)}, u32[]{:S(2)}) copy-start(bf16[520,128]{1,0:T(8,128)(2,1)S(1)} %collective-permute-done.2.refs_3_) | copy-start | bytes 399364
  20.8 11.0 %copy-start.3 = (bf16[520,128]{1,0:T(8,128)(2,1)}, bf16[520,128]{1,0:T(8,128)(2,1)S(1)}, u32[]{:S(2)}) copy-start(bf16[520,128]{1,0:T(8,128)(2,1)S(1)} %collective-permute-done.3.refs_4_) | copy-start | bytes 399364
  31.7 0.7 %copy-start.4 = (bf16[520,128]{1,0:T(8,128)(2,1)}, bf16[520,128]{1,0:T(8,128)(2,1)S(1)}, u32[]{:S(2)}) copy-start(bf16[520,128]{1,0:T(8,128)(2,1)S(1)} %collective-permute-done.4.refs_5_) | copy-start | bytes 399364
  31.7 0.7 %copy-start.5 = (bf16[520,128]{1,0:T(8,128)(2,1)}, bf16[520,128]{1,0:T(8,128)(2,1)S(1)}, u32[]{:S(2)}) copy-start(bf16[520,128]{1,0:T(8,128)(2,1)S(1)} %collective-permute-done.5.refs_6_) | copy-start | bytes 399364
  31.7 0.7 %copy-start.6 = (bf16[520,128]{1,0:T(8,128)(2,1)}, bf16[520,128]{1,0:T(8,128)(2,1)S(1)}, u32[]{:S(2)}) copy-start(bf16[520,128]{1,0:T(8,128)(2,1)S(1)} %collective-permute-done.6.refs_7_) | copy-start | bytes 399364
  39.7 2.1 %collective-permute-start.8 = (f32[1024,128]{1,0:T(8,128)}, f32[1024,128]{1,0:T(8,128)S(1)}, u32[]{:S(2)}, u32[]{:S(2)}) collective-permute-start(f32[1024,128]{1,0:T(8,128)} %get-tuple-element.24), channel_id=1, source_target_pairs={{0,1},{1,0},{2,3},{3,2},{4,5},{5,4},{6,7},{7,6},{8,9},{9,8},{10,11... | collective-permute-start | bytes 1572872 | tf_op jit(solution)/shard_map/ppermute | solution.py:152
  43.0 7.2 %collective-permute-start.9 = (bf16[2,128,128]{2,1,0:T(8,128)(2,1)S(1)}, bf16[2,128,128]{2,1,0:T(8,128)(2,1)S(1)}, u32[]{:S(2)}, u32[]{:S(2)}) collective-permute-start(bf16[2,128,128]{2,1,0:T(8,128)(2,1)S(1)} %get-tuple-element.25), channel_id=1, source_target_pairs={{0,2},{2,0},{4,6},{6,4},{8,10},{10,8},{12,14},{14,12},{1,3},{3,1},... | collective-permute-start | bytes 196616 | tf_op jit(solution)/shard_map/ppermute | solution.py:152
  44.2 8.2 %collective-permute-start.11 = (bf16[2,128,128]{2,1,0:T(8,128)(2,1)S(1)}, bf16[2,128,128]{2,1,0:T(8,128)(2,1)S(1)}, u32[]{:S(2)}, u32[]{:S(2)}) collective-permute-start(bf16[2,128,128]{2,1,0:T(8,128)(2,1)S(1)} %get-tuple-element.26), channel_id=1, source_target_pairs={{0,6},{2,4},{4,2},{6,0},{8,14},{10,12},{12,10},{14,8},{1,7},{3,5},... | collective-permute-start | bytes 196616 | tf_op jit(solution)/shard_map/ppermute | solution.py:152
  50.2 4.3 %collective-permute-start.10 = (bf16[2,128,128]{2,1,0:T(8,128)(2,1)S(1)}, bf16[2,128,128]{2,1,0:T(8,128)(2,1)S(1)}, u32[]{:S(2)}, u32[]{:S(2)}) collective-permute-start(bf16[2,128,128]{2,1,0:T(8,128)(2,1)S(1)} %get-tuple-element.27), channel_id=1, source_target_pairs={{0,4},{2,6},{4,0},{6,2},{8,12},{10,14},{12,8},{14,10},{1,5},{3,7},... | collective-permute-start | bytes 196616 | tf_op jit(solution)/shard_map/ppermute | solution.py:152
  54.5 5.0 %collective-permute-start.12 = (bf16[128,128]{1,0:T(8,128)(2,1)S(1)}, bf16[128,128]{1,0:T(8,128)(2,1)S(1)}, u32[]{:S(2)}, u32[]{:S(2)}) collective-permute-start(bf16[128,128]{1,0:T(8,128)(2,1)S(1)} %fusion.4), channel_id=1, source_target_pairs={{0,8},{2,10},{4,12},{6,14},{8,0},{10,2},{12,4},{14,6},{1,9},{3,11}... | collective-permute-start | bytes 98312 | tf_op jit(solution)/shard_map/ppermute | solution.py:152

commit v2 on v1

--- a/solution.py
+++ b/solution.py
@@ -13,6 +13,13 @@
 LANES = 128
 GROUP = ("gx", "row")
 VMEM = pl.BlockSpec(memory_space=pltpu.VMEM)
+ORDER = (7, 5, 6, 4, 3, 2, 1, 0)
+NEAR = (1, 2, 3)
+PLAIN = ((1,), (0,))
+
+
+def limit(mib):
+    return pltpu.CompilerParams(vmem_limit_bytes=mib << 20)
 
 
 def dot(a, b, dims):
@@ -24,7 +31,8 @@
     return high, (a - high.astype(F32)).astype(BF16)
 
 
-def pack_kernel(peers, feats, *outs):
+def pack_kernel(peers, feats, *ordered):
+    outs = dict(zip(ORDER, ordered))
     ex_dev, modules, feat = feats.shape
     cols = feat // LANES
     step = 256 // modules
@@ -35,18 +43,17 @@
     wanted = ((r // step) ^ me) * lax.axis_size("pb") + side
     pick = ((c // modules == r % step) & (c % modules == wanted)).astype(F32).astype(BF16)
 
-    def body(b, acc):
-        x = feats[pl.ds(b * step, step)].reshape(step * modules, feat)
+    acc = jnp.zeros((8, feat), F32)
+    for b in range(ex_dev // step):
+        x = feats[b * step : (b + 1) * step].reshape(step * modules, feat)
         y = dot(pick, x, ((1,), (0,))).astype(BF16)
         for k in range(peers):
             for j in range(cols):
-                start = pl.multiple_of(j * ex_dev + b * step, step)
-                outs[k][pl.ds(start, step), :] = y[k * step : (k + 1) * step, j * LANES : (j + 1) * LANES]
+                start = j * ex_dev + b * step
+                outs[k][start : start + step, :] = y[k * step : (k + 1) * step, j * LANES : (j + 1) * LANES]
         xf = x.astype(F32)
         sq = xf * xf
-        return acc + sq.reshape(step * modules // 8, 8, feat).sum(0)
-
-    acc = lax.fori_loop(0, ex_dev // step, body, jnp.zeros((8, feat), F32))
+        acc = acc + sq.reshape(step * modules // 8, 8, feat).sum(0)
     lane = acc.sum(0, keepdims=True)
     lane = sum(lane[:, j * LANES : (j + 1) * LANES] for j in range(cols))
     high, rest = split(lane)
@@ -61,13 +68,15 @@
 def pack(features, peers):
     ex_dev, modules, feat = features.shape
     shape = jax.ShapeDtypeStruct((feat // LANES * ex_dev + 8, LANES), BF16)
-    return pl.pallas_call(
+    outs = pl.pallas_call(
         functools.partial(pack_kernel, peers),
         out_shape=[shape] * peers,
         in_specs=[VMEM],
         out_specs=[VMEM] * peers,
+        compiler_params=limit(8),
         name="pack",
     )(features)
+    return dict(zip(ORDER, outs))
 
 
 def pick_kernel(pool, ids, out):
@@ -86,6 +95,7 @@
         out_shape=jax.ShapeDtypeStruct((ids.shape[1], query_pool.shape[2]), BF16),
         in_specs=[VMEM, VMEM],
         out_specs=VMEM,
+        compiler_params=limit(12),
         name="pick",
     )(query_pool, ids)
 
@@ -97,40 +107,39 @@
     ex_dev = count // peers
     cols = feat // LANES
     total = jnp.zeros((1, LANES), F32)
-    for k in range(peers):
+    for k, chunk in zip(ORDER, chunks):
         for j in range(cols):
-            feats[k * ex_dev : (k + 1) * ex_dev, j * LANES : (j + 1) * LANES] = chunks[k][j * ex_dev : (j + 1) * ex_dev, :]
-        total = total + chunks[k][cols * ex_dev :, :].astype(F32).sum(0, keepdims=True)
-    total = jnp.sum(total)
-    damping = 0.5 * total / (count * modules * feat)
+            feats[k * ex_dev : (k + 1) * ex_dev, j * LANES : (j + 1) * LANES] = chunk[j * ex_dev : (j + 1) * ex_dev, :]
+        total = total + chunk[cols * ex_dev :, :].astype(F32).sum(0, keepdims=True)
+    damping = jnp.sum(total, keepdims=True) * (0.5 / (count * modules * feat))
     f = feats[...]
     gram = dot(f, f, ((0,), (0,)))
     diag = lax.broadcasted_iota(jnp.int32, (feat, feat), 0) == lax.broadcasted_iota(jnp.int32, (feat, feat), 1)
-    hessian = gram / count + jnp.where(diag, damping, 0.0)
-    inv = 1.0 / jnp.sqrt(jnp.sum(hessian * hessian) + 1e-06)
-    plain = ((1,), (0,))
+    hessian = gram * (1.0 / count) + jnp.where(diag, damping, 0.0)
+    square = jnp.sum(jnp.sum(hessian * hessian, axis=0, keepdims=True), axis=1, keepdims=True)
+    inv = 1.0 / jnp.sqrt(square + 1e-06)
+    high, low = split(hessian)
 
     def apply(v, mat):
         vh, vl = split(v)
         mh, ml = mat
-        return dot(vh, mh, plain) + (dot(vl, mh, plain) + dot(vh, ml, plain))
-
-    b1 = hessian * inv
-    m1 = split(b1)
-    b2 = 2.0 * b1 - dot(m1[0], m1[0], plain)
+        return dot(vh, mh, PLAIN) + (dot(vl, mh, PLAIN) + dot(vh, ml, PLAIN))
+
+    v = picked[...]
+    b2 = inv * (2.0 * hessian - inv * dot(high, high, PLAIN))
     m2 = split(b2)
-    b4 = 2.0 * b2 - dot(m2[0], m2[0], plain)
+    v = 2.0 * v.astype(F32) - inv * (dot(v, high, PLAIN) + dot(v, low, PLAIN))
+    b4 = 2.0 * b2 - dot(m2[0], m2[0], PLAIN)
     m4 = split(b4)
-    v = picked[...]
-    v = 2.0 * v.astype(F32) - (dot(v, m1[0], plain) + dot(v, m1[1], plain))
     v = 2.0 * v - apply(v, m2)
     v = 2.0 * v - apply(v, m4)
     w = v - apply(v, m4)
     w = w - apply(w, m4)
     precond = ((v + w) * inv).astype(BF16)
     half = precond.shape[0] // 2
-    other[...] = dot(f, precond[half:], ((1,), (1,)))
-    own[...] = dot(f, precond[:half], ((1,), (1,)))
+    scores = dot(f, precond, ((1,), (1,)))
+    other[...] = scores[:, half:]
+    own[...] = scores[:, :half]
 
 
 def score(chunks, picked, modules):
@@ -144,6 +153,7 @@
         in_specs=[VMEM] * (peers + 1),
         out_specs=[VMEM, VMEM],
         scratch_shapes=[pltpu.VMEM((count, feat), BF16)],
+        compiler_params=limit(24),
         name="score",
     )(*chunks, picked)
 
@@ -156,15 +166,16 @@
     ex_dev, modules, feat = features.shape
     peers = lax.axis_size("gx") * lax.axis_size("row")
     ids = jnp.concatenate([query_ids, exchange(query_ids, "pb", 1, 2)])[None, :]
-    chunks = list(pack(features, peers))
-    for k in (6, 7, 4, 5, 2, 3, 1):
+    chunks = pack(features, peers)
+    for k in ORDER[:-1]:
         chunks[k] = exchange(chunks[k], GROUP, k, peers)
+    chunks = [chunks[k] for k in ORDER]
     picked = pick(query_pool, ids)
     own, other = score(chunks, picked, modules)
     part = own + exchange(other, "pb", 1, 2)
     part = part.reshape(2, 4, ex_dev, -1)
     near = part[:, 0]
-    for k in (1, 2, 3):
+    for k in NEAR:
         near = near + exchange(part[:, k].astype(BF16), GROUP, k, peers).astype(F32)
     return near[0] + exchange(near[1].astype(BF16), GROUP, 4, peers).astype(F32)
 

time: 60.4 us -> 49.9 us (0.83)
  Pallas kernels: 14.5 us -> 5.36 us
  waiting for transfers between devices: 19.2 us -> 12.9 us
  starting transfers between devices: 23.2 us -> 29 us
  other arithmetic: 2.35 us -> 0.75 us
  local copies, waits for them, and re-layouts: 0.75 us -> 1.63 us
    ppermute x13, waiting for transfers between devices: 19.2 us -> 12.9 us  [exchange(): return lax.ppermute(x, axes, [(i, i ^ k) for i in range(size)])]
    ppermute x13, starting transfers between devices: 23.2 us -> 29 us  [exchange(): return lax.ppermute(x, axes, [(i, i ^ k) for i in range(size)])]
    pallas_call x1, Pallas kernels: 4.2 us -> 0.45 us  [pack(): pl.pallas_call(functools.partial(pack_kernel, peers), out_shape=[shape] *...]
    pallas_call x1, Pallas kernels: 7.27 us -> 4.16 us  [score(): pl.pallas_call(functools.partial(score_kernel, modules), out_shape=[half,...]
    pallas_call x1, Pallas kernels: 3.04 us -> 0.75 us  [pick(): pl.pallas_call(pick_kernel, out_shape=jax.ShapeDtypeStruct((ids.shape[1],...]
    add x1, other arithmetic: 1.12 us -> 0.08 us  [owned(): part = own + exchange(other, 'pb', 1, 2)]
    unnamed x16 -> x6, local copies, waits for them, and re-layouts: 0.72 us -> 1.6 us
  transfers between devices with their start and end apart: 13 -> 13, of which waited for: 5 -> 7; matrix products, arithmetic and copies ran while one was open for 1% -> 0% of each run, Pallas kernels for 5% -> 2%
where the time goes in v2:
time: 49.9 us; the launch traced here: 49.8 us
  starting transfers between devices  29 us (58%)
  waiting for transfers between devices  12.9 us (26%)
  Pallas kernels  5.36 us (11%)
  local copies, waits for them, and re-layouts  1.63 us (3%)
  other arithmetic  0.75 us (2%)
    ppermute x13, starting transfers between devices, exchange(): return lax.ppermute(x, axes, [(i, i ^ k) for i in range(size)])  29 us
    ppermute x13, waiting for transfers between devices, exchange(): return lax.ppermute(x, axes, [(i, i ^ k) for i in range(size)])  12.9 us
    pallas_call x1, Pallas kernels, score(): pl.pallas_call(functools.partial(score_kernel, modules), out_shape=[half,...  4.16 us
    unnamed x6, local copies, waits for them, and re-layouts  1.6 us
  transfers between devices with their start and end apart: 13, of which 7 were waited for; matrix products, arithmetic and copies ran while one was open for 0% of the time, Pallas kernels for 2%

profile of v2, /device:TPU:0, one launch (start us, length us, event | category | flops | bytes accessed | tf_op | source)
XLA Modules:
  0.0 49.8 jit_solution(7651846759281082205)
XLA Ops:
  0.0 0.0 copy-start
  0.0 1.6 %copy-done = bf16[128,16,512]{2,1,0:T(8,128)(2,1)S(1)} copy-done((bf16[128,16,512]{2,1,0:T(8,128)(2,1)S(1)}, bf16[128,16,512]{2,1,0:T(8,128)(2,1)}, u32[]{:S(2)}) %copy-start) | copy-done | bytes 2097176
  1.6 0.0 copy-start.2
  1.6 0.0 copy-start.1
  1.6 0.5 pack.1
  2.1 6.0 %collective-permute-start = (bf16[520,128]{1,0:T(8,128)(2,1)S(1)}, bf16[520,128]{1,0:T(8,128)(2,1)S(1)}, u32[]{:S(2)}, u32[]{:S(2)}) collective-permute-start(bf16[520,128]{1,0:T(8,128)(2,1)S(1)} %get-tuple-element.15), channel_id=1, source_target_pairs={{0,14},{2,12},{4,10},{6,8},{8,6},{10,4},{12,2},{14,0},{1,15},{3,13... | collective-permute-start | bytes 399368 | tf_op jit(solution)/shard_map/ppermute | solution.py:162
  8.1 0.0 collective-permute-start.1
  8.1 0.0 copy-done.2
  8.1 0.0 collective-permute-start.7
  8.1 1.9 %collective-permute-start.2 = (bf16[520,128]{1,0:T(8,128)(2,1)S(1)}, bf16[520,128]{1,0:T(8,128)(2,1)S(1)}, u32[]{:S(2)}, u32[]{:S(2)}) collective-permute-start(bf16[520,128]{1,0:T(8,128)(2,1)S(1)} %get-tuple-element.17), channel_id=1, source_target_pairs={{0,12},{2,14},{4,8},{6,10},{8,4},{10,6},{12,0},{14,2},{1,13},{3,15... | collective-permute-start | bytes 399368 | tf_op jit(solution)/shard_map/ppermute | solution.py:162
  10.0 1.1 %collective-permute-start.3 = (bf16[520,128]{1,0:T(8,128)(2,1)S(1)}, bf16[520,128]{1,0:T(8,128)(2,1)S(1)}, u32[]{:S(2)}, u32[]{:S(2)}) collective-permute-start(bf16[520,128]{1,0:T(8,128)(2,1)S(1)} %get-tuple-element.18), channel_id=1, source_target_pairs={{0,8},{2,10},{4,12},{6,14},{8,0},{10,2},{12,4},{14,6},{1,9},{3,11}... | collective-permute-start | bytes 399368 | tf_op jit(solution)/shard_map/ppermute | solution.py:162
  11.1 0.0 collective-permute-done.7
  11.1 1.8 %collective-permute-start.4 = (bf16[520,128]{1,0:T(8,128)(2,1)S(1)}, bf16[520,128]{1,0:T(8,128)(2,1)S(1)}, u32[]{:S(2)}, u32[]{:S(2)}) collective-permute-start(bf16[520,128]{1,0:T(8,128)(2,1)S(1)} %get-tuple-element.19), channel_id=1, source_target_pairs={{0,6},{2,4},{4,2},{6,0},{8,14},{10,12},{12,10},{14,8},{1,7},{3,5},... | collective-permute-start | bytes 399368 | tf_op jit(solution)/shard_map/ppermute | solution.py:162
  12.8 0.0 collective-permute-done.refs_0_
  12.8 11.3 %collective-permute-start.5 = (bf16[520,128]{1,0:T(8,128)(2,1)S(1)}, bf16[520,128]{1,0:T(8,128)(2,1)S(1)}, u32[]{:S(2)}, u32[]{:S(2)}) collective-permute-start(bf16[520,128]{1,0:T(8,128)(2,1)S(1)} %get-tuple-element.20), channel_id=1, source_target_pairs={{0,4},{2,6},{4,0},{6,2},{8,12},{10,14},{12,8},{14,10},{1,5},{3,7},... | collective-permute-start | bytes 399368 | tf_op jit(solution)/shard_map/ppermute | solution.py:162
  24.1 1.9 %collective-permute-done.1.refs_1_ = bf16[520,128]{1,0:T(8,128)(2,1)S(1)} collective-permute-done((bf16[520,128]{1,0:T(8,128)(2,1)S(1)}, bf16[520,128]{1,0:T(8,128)(2,1)S(1)}, u32[]{:S(2)}, u32[]{:S(2)}) %collective-permute-start.1) | collective-permute-done | bytes 133152 | tf_op jit(solution)/shard_map/ppermute | solution.py:162
  26.0 1.4 %collective-permute-start.6 = (bf16[520,128]{1,0:T(8,128)(2,1)S(1)}, bf16[520,128]{1,0:T(8,128)(2,1)S(1)}, u32[]{:S(2)}, u32[]{:S(2)}) collective-permute-start(bf16[520,128]{1,0:T(8,128)(2,1)S(1)} %get-tuple-element.21), channel_id=1, source_target_pairs={{0,2},{2,0},{4,6},{6,4},{8,10},{10,8},{12,14},{14,12},{1,3},{3,1},... | collective-permute-start | bytes 399368 | tf_op jit(solution)/shard_map/ppermute | solution.py:162
  27.5 0.0 copy-done.1
  27.5 0.8 %pick.1.refs_8_ = bf16[256,512]{1,0:T(8,128)(2,1)S(1)} custom-call(bf16[512,4,512]{2,1,0:T(4,128)(2,1)S(1)} %copy-done.1, s32[1,256]{1,0:T(1,128)S(1)} %bitcast.22), custom_call_target="tpu_custom_call" | custom-call | tf_op jit(solution)/shard_map/pick/pallas_call | solution.py:93
  28.2 0.0 collective-permute-done.2.refs_2_
  28.2 2.6 %collective-permute-done.3.refs_3_ = bf16[520,128]{1,0:T(8,128)(2,1)S(1)} collective-permute-done((bf16[520,128]{1,0:T(8,128)(2,1)S(1)}, bf16[520,128]{1,0:T(8,128)(2,1)S(1)}, u32[]{:S(2)}, u32[]{:S(2)}) %collective-permute-start.3) | collective-permute-done | bytes 133152 | tf_op jit(solution)/shard_map/ppermute | solution.py:162
  30.8 0.0 collective-permute-done.4.refs_4_
  30.8 0.0 collective-permute-done.5.refs_5_
  30.8 0.2 collective-permute-done.6.refs_6_
  31.0 4.2 %score.1 = (f32[1024,128]{1,0:T(8,128)S(1)}, f32[1024,128]{1,0:T(8,128)S(1)}) custom-call(bf16[520,128]{1,0:T(8,128)(2,1)S(1)} %collective-permute-done.refs_0_, bf16[520,128]{1,0:T(8,128)(2,1)S(1)} %collective-permute-done.1.refs_1_, bf16[520,128]{1,0:T(8,128)(2,1)S(1)} %collective-permute-done.2.refs_2_, ...), custom_call_target="tpu_custom_call" | custom-call | tf_op jit(solution)/shard_map/score/pallas_call | solution.py:150
  35.2 0.1 collective-permute-start.8
  35.2 1.9 %collective-permute-done.8 = f32[1024,128]{1,0:T(8,128)S(1)} collective-permute-done((f32[1024,128]{1,0:T(8,128)S(1)}, f32[1024,128]{1,0:T(8,128)S(1)}, u32[]{:S(2)}, u32[]{:S(2)}) %collective-permute-start.8) | collective-permute-done | bytes 524320 | tf_op jit(solution)/shard_map/ppermute | solution.py:162
  37.1 0.1 add.15
  37.3 1.5 %collective-permute-start.9 = (bf16[2,128,128]{2,1,0:T(8,128)(2,1)S(1)}, bf16[2,128,128]{2,1,0:T(8,128)(2,1)S(1)}, u32[]{:S(2)}, u32[]{:S(2)}) collective-permute-start(bf16[2,128,128]{2,1,0:T(8,128)(2,1)S(1)} %get-tuple-element.25), channel_id=1, source_target_pairs={{0,2},{2,0},{4,6},{6,4},{8,10},{10,8},{12,14},{14,12},{1,3},{3,1},... | collective-permute-start | bytes 196616 | tf_op jit(solution)/shard_map/ppermute | solution.py:162
  38.8 0.0 collective-permute-start.11
  38.8 2.0 %collective-permute-start.10 = (bf16[2,128,128]{2,1,0:T(8,128)(2,1)S(1)}, bf16[2,128,128]{2,1,0:T(8,128)(2,1)S(1)}, u32[]{:S(2)}, u32[]{:S(2)}) collective-permute-start(bf16[2,128,128]{2,1,0:T(8,128)(2,1)S(1)} %get-tuple-element.27), channel_id=1, source_target_pairs={{0,4},{2,6},{4,0},{6,2},{8,12},{10,14},{12,8},{14,10},{1,5},{3,7},... | collective-permute-start | bytes 196616 | tf_op jit(solution)/shard_map/ppermute | solution.py:162
  40.8 0.8 %collective-permute-done.9 = bf16[2,128,128]{2,1,0:T(8,128)(2,1)S(1)} collective-permute-done((bf16[2,128,128]{2,1,0:T(8,128)(2,1)S(1)}, bf16[2,128,128]{2,1,0:T(8,128)(2,1)S(1)}, u32[]{:S(2)}, u32[]{:S(2)}) %collective-permute-start.9) | collective-permute-done | bytes 65568 | tf_op jit(solution)/shard_map/ppermute | solution.py:162
  41.6 2.6 %collective-permute-done.11 = bf16[2,128,128]{2,1,0:T(8,128)(2,1)S(1)} collective-permute-done((bf16[2,128,128]{2,1,0:T(8,128)(2,1)S(1)}, bf16[2,128,128]{2,1,0:T(8,128)(2,1)S(1)}, u32[]{:S(2)}, u32[]{:S(2)}) %collective-permute-start.11) | collective-permute-done | bytes 65568 | tf_op jit(solution)/shard_map/ppermute | solution.py:162
  44.2 0.0 collective-permute-done.10
  44.3 1.9 %collective-permute-start.12 = (bf16[128,128]{1,0:T(8,128)(2,1)S(1)}, bf16[128,128]{1,0:T(8,128)(2,1)S(1)}, u32[]{:S(2)}, u32[]{:S(2)}) collective-permute-start(bf16[128,128]{1,0:T(8,128)(2,1)S(1)} %fusion.4), channel_id=1, source_target_pairs={{0,8},{2,10},{4,12},{6,14},{8,0},{10,2},{12,4},{14,6},{1,9},{3,11}... | collective-permute-start | bytes 98312 | tf_op jit(solution)/shard_map/ppermute | solution.py:162
  46.2 2.9 %collective-permute-done.12 = bf16[128,128]{1,0:T(8,128)(2,1)S(1)} collective-permute-done((bf16[128,128]{1,0:T(8,128)(2,1)S(1)}, bf16[128,128]{1,0:T(8,128)(2,1)S(1)}, u32[]{:S(2)}, u32[]{:S(2)}) %collective-permute-start.12) | collective-permute-done | bytes 32800 | tf_op jit(solution)/shard_map/ppermute | solution.py:162
  49.2 0.6 %fusion.3 = f32[128,128]{1,0:T(8,128)} fusion(f32[2,128,128]{2,1,0:T(8,128)S(1)} %fusion.2, bf16[128,128]{1,0:T(8,128)(2,1)S(1)} %collective-permute-done.12), kind=kLoop, calls=%fused_computation.6 | loop fusion | flops 32768 | bytes 163840 | tf_op jit(solution)/shard_map/add | solution.py:180
  (4 shorter events, 0.1 us)
Async XLA Ops:
  0.0 1.6 %copy-start = (bf16[128,16,512]{2,1,0:T(8,128)(2,1)S(1)}, bf16[128,16,512]{2,1,0:T(8,128)(2,1)}, u32[]{:S(2)}) copy-start(bf16[128,16,512]{2,1,0:T(8,128)(2,1)} %feats.1) | copy-start | bytes 6291460
  1.6 6.5 %copy-start.2 = (s32[128]{0:T(128)S(1)}, s32[128]{0:T(128)}, u32[]{:S(2)}) copy-start(s32[128]{0:T(128)} %param.5) | copy-start | bytes 1540
  1.6 25.9 %copy-start.1 = (bf16[512,4,512]{2,1,0:T(4,128)(2,1)S(1)}, bf16[512,4,512]{2,1,0:T(4,128)(2,1)}, u32[]{:S(2)}) copy-start(bf16[512,4,512]{2,1,0:T(4,128)(2,1)} %pool.1) | copy-start | bytes 6291460
  2.1 10.8 %collective-permute-start = (bf16[520,128]{1,0:T(8,128)(2,1)S(1)}, bf16[520,128]{1,0:T(8,128)(2,1)S(1)}, u32[]{:S(2)}, u32[]{:S(2)}) collective-permute-start(bf16[520,128]{1,0:T(8,128)(2,1)S(1)} %get-tuple-element.15), channel_id=1, source_target_pairs={{0,14},{2,12},{4,10},{6,8},{8,6},{10,4},{12,2},{14,0},{1,15},{3,13... | collective-permute-start | bytes 399368 | tf_op jit(solution)/shard_map/ppermute | solution.py:162
  8.1 17.9 %collective-permute-start.1 = (bf16[520,128]{1,0:T(8,128)(2,1)S(1)}, bf16[520,128]{1,0:T(8,128)(2,1)S(1)}, u32[]{:S(2)}, u32[]{:S(2)}) collective-permute-start(bf16[520,128]{1,0:T(8,128)(2,1)S(1)} %get-tuple-element.16), channel_id=1, source_target_pairs={{0,10},{2,8},{4,14},{6,12},{8,2},{10,0},{12,6},{14,4},{1,11},{3,9}... | collective-permute-start | bytes 399368 | tf_op jit(solution)/shard_map/ppermute | solution.py:162
  8.1 3.0 %collective-permute-start.7 = (s32[128]{0:T(128)S(1)}, s32[128]{0:T(128)S(1)}, u32[]{:S(2)}, u32[]{:S(2)}) collective-permute-start(s32[128]{0:T(128)S(1)} %copy-done.2), channel_id=1, source_target_pairs={{0,1},{1,0},{2,3},{3,2},{4,5},{5,4},{6,7},{7,6},{8,9},{9,8},{10,11... | collective-permute-start | bytes 1544 | tf_op jit(solution)/shard_map/ppermute | solution.py:162
  8.1 20.1 %collective-permute-start.2 = (bf16[520,128]{1,0:T(8,128)(2,1)S(1)}, bf16[520,128]{1,0:T(8,128)(2,1)S(1)}, u32[]{:S(2)}, u32[]{:S(2)}) collective-permute-start(bf16[520,128]{1,0:T(8,128)(2,1)S(1)} %get-tuple-element.17), channel_id=1, source_target_pairs={{0,12},{2,14},{4,8},{6,10},{8,4},{10,6},{12,0},{14,2},{1,13},{3,15... | collective-permute-start | bytes 399368 | tf_op jit(solution)/shard_map/ppermute | solution.py:162
  10.0 20.8 %collective-permute-start.3 = (bf16[520,128]{1,0:T(8,128)(2,1)S(1)}, bf16[520,128]{1,0:T(8,128)(2,1)S(1)}, u32[]{:S(2)}, u32[]{:S(2)}) collective-permute-start(bf16[520,128]{1,0:T(8,128)(2,1)S(1)} %get-tuple-element.18), channel_id=1, source_target_pairs={{0,8},{2,10},{4,12},{6,14},{8,0},{10,2},{12,4},{14,6},{1,9},{3,11}... | collective-permute-start | bytes 399368 | tf_op jit(solution)/shard_map/ppermute | solution.py:162
  11.1 19.7 %collective-permute-start.4 = (bf16[520,128]{1,0:T(8,128)(2,1)S(1)}, bf16[520,128]{1,0:T(8,128)(2,1)S(1)}, u32[]{:S(2)}, u32[]{:S(2)}) collective-permute-start(bf16[520,128]{1,0:T(8,128)(2,1)S(1)} %get-tuple-element.19), channel_id=1, source_target_pairs={{0,6},{2,4},{4,2},{6,0},{8,14},{10,12},{12,10},{14,8},{1,7},{3,5},... | collective-permute-start | bytes 399368 | tf_op jit(solution)/shard_map/ppermute | solution.py:162
  12.8 18.0 %collective-permute-start.5 = (bf16[520,128]{1,0:T(8,128)(2,1)S(1)}, bf16[520,128]{1,0:T(8,128)(2,1)S(1)}, u32[]{:S(2)}, u32[]{:S(2)}) collective-permute-start(bf16[520,128]{1,0:T(8,128)(2,1)S(1)} %get-tuple-element.20), channel_id=1, source_target_pairs={{0,4},{2,6},{4,0},{6,2},{8,12},{10,14},{12,8},{14,10},{1,5},{3,7},... | collective-permute-start | bytes 399368 | tf_op jit(solution)/shard_map/ppermute | solution.py:162
  26.0 5.0 %collective-permute-start.6 = (bf16[520,128]{1,0:T(8,128)(2,1)S(1)}, bf16[520,128]{1,0:T(8,128)(2,1)S(1)}, u32[]{:S(2)}, u32[]{:S(2)}) collective-permute-start(bf16[520,128]{1,0:T(8,128)(2,1)S(1)} %get-tuple-element.21), channel_id=1, source_target_pairs={{0,2},{2,0},{4,6},{6,4},{8,10},{10,8},{12,14},{14,12},{1,3},{3,1},... | collective-permute-start | bytes 399368 | tf_op jit(solution)/shard_map/ppermute | solution.py:162
  35.2 2.0 %collective-permute-start.8 = (f32[1024,128]{1,0:T(8,128)S(1)}, f32[1024,128]{1,0:T(8,128)S(1)}, u32[]{:S(2)}, u32[]{:S(2)}) collective-permute-start(f32[1024,128]{1,0:T(8,128)S(1)} %get-tuple-element.24), channel_id=1, source_target_pairs={{0,1},{1,0},{2,3},{3,2},{4,5},{5,4},{6,7},{7,6},{8,9},{9,8},{10,11... | collective-permute-start | bytes 1572872 | tf_op jit(solution)/shard_map/ppermute | solution.py:162
  37.3 4.3 %collective-permute-start.9 = (bf16[2,128,128]{2,1,0:T(8,128)(2,1)S(1)}, bf16[2,128,128]{2,1,0:T(8,128)(2,1)S(1)}, u32[]{:S(2)}, u32[]{:S(2)}) collective-permute-start(bf16[2,128,128]{2,1,0:T(8,128)(2,1)S(1)} %get-tuple-element.25), channel_id=1, source_target_pairs={{0,2},{2,0},{4,6},{6,4},{8,10},{10,8},{12,14},{14,12},{1,3},{3,1},... | collective-permute-start | bytes 196616 | tf_op jit(solution)/shard_map/ppermute | solution.py:162
  38.8 5.5 %collective-permute-start.11 = (bf16[2,128,128]{2,1,0:T(8,128)(2,1)S(1)}, bf16[2,128,128]{2,1,0:T(8,128)(2,1)S(1)}, u32[]{:S(2)}, u32[]{:S(2)}) collective-permute-start(bf16[2,128,128]{2,1,0:T(8,128)(2,1)S(1)} %get-tuple-element.26), channel_id=1, source_target_pairs={{0,6},{2,4},{4,2},{6,0},{8,14},{10,12},{12,10},{14,8},{1,7},{3,5},... | collective-permute-start | bytes 196616 | tf_op jit(solution)/shard_map/ppermute | solution.py:162
  38.8 5.5 %collective-permute-start.10 = (bf16[2,128,128]{2,1,0:T(8,128)(2,1)S(1)}, bf16[2,128,128]{2,1,0:T(8,128)(2,1)S(1)}, u32[]{:S(2)}, u32[]{:S(2)}) collective-permute-start(bf16[2,128,128]{2,1,0:T(8,128)(2,1)S(1)} %get-tuple-element.27), channel_id=1, source_target_pairs={{0,4},{2,6},{4,0},{6,2},{8,12},{10,14},{12,8},{14,10},{1,5},{3,7},... | collective-permute-start | bytes 196616 | tf_op jit(solution)/shard_map/ppermute | solution.py:162
  44.3 4.9 %collective-permute-start.12 = (bf16[128,128]{1,0:T(8,128)(2,1)S(1)}, bf16[128,128]{1,0:T(8,128)(2,1)S(1)}, u32[]{:S(2)}, u32[]{:S(2)}) collective-permute-start(bf16[128,128]{1,0:T(8,128)(2,1)S(1)} %fusion.4), channel_id=1, source_target_pairs={{0,8},{2,10},{4,12},{6,14},{8,0},{10,2},{12,4},{14,6},{1,9},{3,11}... | collective-permute-start | bytes 98312 | tf_op jit(solution)/shard_map/ppermute | solution.py:162

commit v3 on v2

--- a/solution.py
+++ b/solution.py
@@ -13,8 +13,9 @@
 LANES = 128
 GROUP = ("gx", "row")
 VMEM = pl.BlockSpec(memory_space=pltpu.VMEM)
-ORDER = (7, 5, 6, 4, 3, 2, 1, 0)
-NEAR = (1, 2, 3)
+ORDER = (6, 5, 7, 4, 3, 2, 1, 0)
+LATE = (4, 1)
+NEAR = (2, 3, 1)
 PLAIN = ((1,), (0,))
 
 
@@ -100,20 +101,53 @@
     )(query_pool, ids)
 
 
-def score_kernel(modules, *refs):
-    peers = len(refs) - 4
-    chunks, (picked, own, other, feats) = refs[:peers], refs[peers:]
-    count, feat = feats.shape
-    ex_dev = count // peers
-    cols = feat // LANES
+def assemble(chunks, feats):
+    ex_dev = feats.shape[0] // len(chunks)
+    cols = feats.shape[1] // LANES
     total = jnp.zeros((1, LANES), F32)
-    for k, chunk in zip(ORDER, chunks):
+    for k, chunk in enumerate(chunks):
         for j in range(cols):
             feats[k * ex_dev : (k + 1) * ex_dev, j * LANES : (j + 1) * LANES] = chunk[j * ex_dev : (j + 1) * ex_dev, :]
         total = total + chunk[cols * ex_dev :, :].astype(F32).sum(0, keepdims=True)
+    return total
+
+
+def early_kernel(*refs):
+    *chunks, feats, gram, total = refs
+    total[...] = jnp.broadcast_to(assemble(chunks, feats), total.shape)
+    f = feats[...]
+    gram[...] = dot(f, f, ((0,), (0,)))
+
+
+def cost(flops):
+    return pl.CostEstimate(flops=int(flops), bytes_accessed=1 << 22, transcendentals=0)
+
+
+def early(chunks, feat):
+    count = len(chunks) * (chunks[0].shape[0] - 8) * LANES // feat
+    return pl.pallas_call(
+        early_kernel,
+        out_shape=[
+            jax.ShapeDtypeStruct((count, feat), BF16),
+            jax.ShapeDtypeStruct((feat, feat), F32),
+            jax.ShapeDtypeStruct((8, LANES), F32),
+        ],
+        in_specs=[VMEM] * len(chunks),
+        out_specs=[VMEM] * 3,
+        compiler_params=limit(16),
+        cost_estimate=cost(2 * count * feat * feat),
+        name="early",
+    )(*chunks)
+
+
+def score_kernel(modules, *refs):
+    *chunks, early_feats, early_gram, early_total, picked, own, other, feats = refs
+    ahead, feat = early_feats.shape
+    count = ahead + feats.shape[0]
+    total = early_total[0:1, :] + assemble(chunks, feats)
     damping = jnp.sum(total, keepdims=True) * (0.5 / (count * modules * feat))
     f = feats[...]
-    gram = dot(f, f, ((0,), (0,)))
+    gram = early_gram[...] + dot(f, f, ((0,), (0,)))
     diag = lax.broadcasted_iota(jnp.int32, (feat, feat), 0) == lax.broadcasted_iota(jnp.int32, (feat, feat), 1)
     hessian = gram * (1.0 / count) + jnp.where(diag, damping, 0.0)
     square = jnp.sum(jnp.sum(hessian * hessian, axis=0, keepdims=True), axis=1, keepdims=True)
@@ -128,7 +162,7 @@
     v = picked[...]
     b2 = inv * (2.0 * hessian - inv * dot(high, high, PLAIN))
     m2 = split(b2)
-    v = 2.0 * v.astype(F32) - inv * (dot(v, high, PLAIN) + dot(v, low, PLAIN))
+    v = 2.0 * v.astype(F32) - inv * dot(v, high, PLAIN)
     b4 = 2.0 * b2 - dot(m2[0], m2[0], PLAIN)
     m4 = split(b4)
     v = 2.0 * v - apply(v, m2)
@@ -137,25 +171,26 @@
     w = w - apply(w, m4)
     precond = ((v + w) * inv).astype(BF16)
     half = precond.shape[0] // 2
-    scores = dot(f, precond, ((1,), (1,)))
-    other[...] = scores[:, half:]
-    own[...] = scores[:, :half]
-
-
-def score(chunks, picked, modules):
-    peers = len(chunks)
+    for rows, block in ((slice(0, ahead), early_feats[...]), (slice(ahead, count), f)):
+        scores = dot(block, precond, ((1,), (1,)))
+        other[rows, :] = scores[:, half:]
+        own[rows, :] = scores[:, :half]
+
+
+def score(late, ahead, picked, modules):
     queries, feat = picked.shape
-    count = peers * (chunks[0].shape[0] - 8) * LANES // feat
+    late_count = len(late) * (late[0].shape[0] - 8) * LANES // feat
+    count = ahead[0].shape[0] + late_count
     half = jax.ShapeDtypeStruct((count, queries // 2), F32)
     return pl.pallas_call(
         functools.partial(score_kernel, modules),
         out_shape=[half, half],
-        in_specs=[VMEM] * (peers + 1),
+        in_specs=[VMEM] * (len(late) + 4),
         out_specs=[VMEM, VMEM],
-        scratch_shapes=[pltpu.VMEM((count, feat), BF16)],
+        scratch_shapes=[pltpu.VMEM((late_count, feat), BF16)],
         compiler_params=limit(24),
         name="score",
-    )(*chunks, picked)
+    )(*late, *ahead, picked)
 
 
 def exchange(x, axes, k, size):
@@ -169,14 +204,17 @@
     chunks = pack(features, peers)
     for k in ORDER[:-1]:
         chunks[k] = exchange(chunks[k], GROUP, k, peers)
-    chunks = [chunks[k] for k in ORDER]
     picked = pick(query_pool, ids)
-    own, other = score(chunks, picked, modules)
+    first = [k for k in ORDER if k not in LATE]
+    ahead = early([chunks[k] for k in first], feat)
+    own, other = score([chunks[k] for k in LATE], ahead, picked, modules)
     part = own + exchange(other, "pb", 1, 2)
-    part = part.reshape(2, 4, ex_dev, -1)
-    near = part[:, 0]
+    part = part.reshape(peers, ex_dev, -1)
+    place = {k: i for i, k in enumerate(first + list(LATE))}
+    pair = lambda k: jnp.stack([part[place[k]], part[place[k + 4]]])
+    near = pair(0)
     for k in NEAR:
-        near = near + exchange(part[:, k].astype(BF16), GROUP, k, peers).astype(F32)
+        near = near + exchange(pair(k).astype(BF16), GROUP, k, peers).astype(F32)
     return near[0] + exchange(near[1].astype(BF16), GROUP, 4, peers).astype(F32)
 
 

time: 49.9 us -> 47.8 us (0.958)
  starting transfers between devices: 29 us -> 25.1 us
  waiting for transfers between devices: 12.9 us -> 14.6 us
    ppermute x13, starting transfers between devices: 29 us -> 25.1 us  [exchange(): return lax.ppermute(x, axes, [(i, i ^ k) for i in range(size)])]
    ppermute x13, waiting for transfers between devices: 12.9 us -> 14.6 us  [exchange(): return lax.ppermute(x, axes, [(i, i ^ k) for i in range(size)])]
    pallas_call x0 -> x1, Pallas kernels: none -> 0.66 us  [early(): pl.pallas_call(early_kernel, out_shape=[jax.ShapeDtypeStruct((count, feat...]
    pallas_call x1, Pallas kernels: 4.16 us -> 3.6 us  [score(): pl.pallas_call(functools.partial(score_kernel, modules), out_shape=[half,...]
  transfers between devices with their start and end apart: 13 -> 13, of which waited for: 7 -> 7; matrix products, arithmetic and copies ran while one was open for 0% -> 0% of each run, Pallas kernels for 2% -> 3%
where the time goes in v3:
time: 47.8 us; the launch traced here: 47.7 us
  starting transfers between devices  25.1 us (53%)
  waiting for transfers between devices  14.6 us (31%)
  Pallas kernels  5.47 us (11%)
  local copies, waits for them, and re-layouts  1.63 us (3%)
  other arithmetic  0.83 us (2%)
    ppermute x13, starting transfers between devices, exchange(): return lax.ppermute(x, axes, [(i, i ^ k) for i in range(size)])  25.1 us
    ppermute x13, waiting for transfers between devices, exchange(): return lax.ppermute(x, axes, [(i, i ^ k) for i in range(size)])  14.6 us
    pallas_call x1, Pallas kernels, score(): pl.pallas_call(functools.partial(score_kernel, modules), out_shape=[half,...  3.6 us
    unnamed x6, local copies, waits for them, and re-layouts  1.6 us
  transfers between devices with their start and end apart: 13, of which 7 were waited for; matrix products, arithmetic and copies ran while one was open for 0% of the time, Pallas kernels for 3%

profile of v3, /device:TPU:0, one launch (start us, length us, event | category | flops | bytes accessed | tf_op | source)
XLA Modules:
  0.0 47.7 jit_solution(5608892933833275057)
XLA Ops:
  0.0 0.0 copy-start
  0.0 1.6 %copy-done = bf16[128,16,512]{2,1,0:T(8,128)(2,1)S(1)} copy-done((bf16[128,16,512]{2,1,0:T(8,128)(2,1)S(1)}, bf16[128,16,512]{2,1,0:T(8,128)(2,1)}, u32[]{:S(2)}) %copy-start) | copy-done | bytes 2097176
  1.6 0.0 copy-start.2
  1.6 0.0 copy-start.1
  1.6 0.5 pack.1
  2.1 5.1 %collective-permute-start.2 = (bf16[520,128]{1,0:T(8,128)(2,1)S(1)}, bf16[520,128]{1,0:T(8,128)(2,1)S(1)}, u32[]{:S(2)}, u32[]{:S(2)}) collective-permute-start(bf16[520,128]{1,0:T(8,128)(2,1)S(1)} %get-tuple-element.20), channel_id=1, source_target_pairs={{0,12},{2,14},{4,8},{6,10},{8,4},{10,6},{12,0},{14,2},{1,13},{3,15... | collective-permute-start | bytes 399368 | tf_op jit(solution)/shard_map/ppermute | solution.py:197
  7.2 0.4 collective-permute-start.3
  7.5 0.0 copy-done.2
  7.5 0.0 collective-permute-start.7
  7.5 2.4 %collective-permute-start.4 = (bf16[520,128]{1,0:T(8,128)(2,1)S(1)}, bf16[520,128]{1,0:T(8,128)(2,1)S(1)}, u32[]{:S(2)}, u32[]{:S(2)}) collective-permute-start(bf16[520,128]{1,0:T(8,128)(2,1)S(1)} %get-tuple-element.22), channel_id=1, source_target_pairs={{0,14},{2,12},{4,10},{6,8},{8,6},{10,4},{12,2},{14,0},{1,15},{3,13... | collective-permute-start | bytes 399368 | tf_op jit(solution)/shard_map/ppermute | solution.py:197
  10.0 2.5 %collective-permute-start.5 = (bf16[520,128]{1,0:T(8,128)(2,1)S(1)}, bf16[520,128]{1,0:T(8,128)(2,1)S(1)}, u32[]{:S(2)}, u32[]{:S(2)}) collective-permute-start(bf16[520,128]{1,0:T(8,128)(2,1)S(1)} %get-tuple-element.23), channel_id=1, source_target_pairs={{0,6},{2,4},{4,2},{6,0},{8,14},{10,12},{12,10},{14,8},{1,7},{3,5},... | collective-permute-start | bytes 399368 | tf_op jit(solution)/shard_map/ppermute | solution.py:197
  12.5 0.0 collective-permute-done.7
  12.5 0.5 collective-permute-start.6
  12.9 0.0 collective-permute-done.2.refs_0_
  13.0 7.9 %collective-permute-start = (bf16[520,128]{1,0:T(8,128)(2,1)S(1)}, bf16[520,128]{1,0:T(8,128)(2,1)S(1)}, u32[]{:S(2)}, u32[]{:S(2)}) collective-permute-start(bf16[520,128]{1,0:T(8,128)(2,1)S(1)} %get-tuple-element.18), channel_id=1, source_target_pairs={{0,8},{2,10},{4,12},{6,14},{8,0},{10,2},{12,4},{14,6},{1,9},{3,11}... | collective-permute-start | bytes 399368 | tf_op jit(solution)/shard_map/ppermute | solution.py:197
  20.9 3.3 %collective-permute-done.3.refs_1_ = bf16[520,128]{1,0:T(8,128)(2,1)S(1)} collective-permute-done((bf16[520,128]{1,0:T(8,128)(2,1)S(1)}, bf16[520,128]{1,0:T(8,128)(2,1)S(1)}, u32[]{:S(2)}, u32[]{:S(2)}) %collective-permute-start.3) | collective-permute-done | bytes 133152 | tf_op jit(solution)/shard_map/ppermute | solution.py:197
  24.2 0.0 collective-permute-start.1
  24.3 0.0 copy-done.1
  24.3 0.8 %pick.1.refs_5_ = bf16[256,512]{1,0:T(8,128)(2,1)S(1)} custom-call(bf16[512,4,512]{2,1,0:T(4,128)(2,1)S(1)} %copy-done.1, s32[1,256]{1,0:T(1,128)S(1)} %bitcast.23), custom_call_target="tpu_custom_call" | custom-call | tf_op jit(solution)/shard_map/pick/pallas_call | solution.py:94
  25.0 0.0 collective-permute-done.4.refs_2_
  25.0 0.0 collective-permute-done.5.refs_3_
  25.1 0.0 collective-permute-done.6.refs_4_
  25.1 0.7 %early.1 = (bf16[768,512]{1,0:T(8,128)(2,1)S(1)}, f32[512,512]{1,0:T(8,128)S(1)}, f32[8,128]{1,0:T(8,128)S(1)}) custom-call(bf16[520,128]{1,0:T(8,128)(2,1)S(1)} %collective-permute-done.2.refs_0_, bf16[520,128]{1,0:T(8,128)(2,1)S(1)} %collective-permute-done.3.refs_1_, bf16[520,128]{1,0:T(8,128)(2,1)S(1)} %collective-permute-done.4.refs_2_, ...), custom_call_target="tpu_custom_call" | custom-call | flops 402653184 | bytes 4194304 | tf_op jit(solution)/shard_map/early/pallas_call | solution.py:128
  25.7 4.1 %collective-permute-done.refs_0_ = bf16[520,128]{1,0:T(8,128)(2,1)S(1)} collective-permute-done((bf16[520,128]{1,0:T(8,128)(2,1)S(1)}, bf16[520,128]{1,0:T(8,128)(2,1)S(1)}, u32[]{:S(2)}, u32[]{:S(2)}) %collective-permute-start) | collective-permute-done | bytes 133152 | tf_op jit(solution)/shard_map/ppermute | solution.py:197
  29.8 0.0 collective-permute-done.1.refs_1_
  29.8 3.6 %score.1 = (f32[1024,128]{1,0:T(8,128)S(1)}, f32[1024,128]{1,0:T(8,128)S(1)}) custom-call(bf16[520,128]{1,0:T(8,128)(2,1)S(1)} %collective-permute-done.refs_0_, bf16[520,128]{1,0:T(8,128)(2,1)S(1)} %collective-permute-done.1.refs_1_, bf16[768,512]{1,0:T(8,128)(2,1)S(1)} %get-tuple-element.26.refs_2_, f32[512,512]{1,0:T(8,128)S(1)} %get-tuple-element.27.refs_3_, ...), custom_call_target="tpu_custom_call" | custom-call | tf_op jit(solution)/shard_map/score/pallas_call | solution.py:185
  33.4 0.1 collective-permute-start.8
  33.5 1.9 %collective-permute-done.8 = f32[1024,128]{1,0:T(8,128)S(1)} collective-permute-done((f32[1024,128]{1,0:T(8,128)S(1)}, f32[1024,128]{1,0:T(8,128)S(1)}, u32[]{:S(2)}, u32[]{:S(2)}) %collective-permute-start.8) | collective-permute-done | bytes 524320 | tf_op jit(solution)/shard_map/ppermute | solution.py:197
  35.4 0.1 fusion.4
  35.6 0.6 %collective-permute-start.10 = (bf16[2,128,128]{2,1,0:T(8,128)(2,1)S(1)}, bf16[2,128,128]{2,1,0:T(8,128)(2,1)S(1)}, u32[]{:S(2)}, u32[]{:S(2)}) collective-permute-start(bf16[2,128,128]{2,1,0:T(8,128)(2,1)S(1)} %pad_maximum_fusion.1), channel_id=1, source_target_pairs={{0,6},{2,4},{4,2},{6,0},{8,14},{10,12},{12,10},{14,8},{1,7},{3,5},... | collective-permute-start | bytes 196616 | tf_op jit(solution)/shard_map/ppermute | solution.py:197
  36.2 1.2 %collective-permute-start.11 = (bf16[2,128,128]{2,1,0:T(8,128)(2,1)S(1)}, bf16[2,128,128]{2,1,0:T(8,128)(2,1)S(1)}, u32[]{:S(2)}, u32[]{:S(2)}) collective-permute-start(bf16[2,128,128]{2,1,0:T(8,128)(2,1)S(1)} %pad_maximum_fusion.2), channel_id=1, source_target_pairs={{0,2},{2,0},{4,6},{6,4},{8,10},{10,8},{12,14},{14,12},{1,3},{3,1},... | collective-permute-start | bytes 196616 | tf_op jit(solution)/shard_map/ppermute | solution.py:197
  37.5 1.8 %collective-permute-start.9 = (bf16[2,128,128]{2,1,0:T(8,128)(2,1)S(1)}, bf16[2,128,128]{2,1,0:T(8,128)(2,1)S(1)}, u32[]{:S(2)}, u32[]{:S(2)}) collective-permute-start(bf16[2,128,128]{2,1,0:T(8,128)(2,1)S(1)} %pad_maximum_fusion), channel_id=1, source_target_pairs={{0,4},{2,6},{4,0},{6,2},{8,12},{10,14},{12,8},{14,10},{1,5},{3,7},... | collective-permute-start | bytes 196616 | tf_op jit(solution)/shard_map/ppermute | solution.py:197
  39.3 1.8 %collective-permute-done.10 = bf16[2,128,128]{2,1,0:T(8,128)(2,1)S(1)} collective-permute-done((bf16[2,128,128]{2,1,0:T(8,128)(2,1)S(1)}, bf16[2,128,128]{2,1,0:T(8,128)(2,1)S(1)}, u32[]{:S(2)}, u32[]{:S(2)}) %collective-permute-start.10) | collective-permute-done | bytes 65568 | tf_op jit(solution)/shard_map/ppermute | solution.py:197
  41.1 0.5 collective-permute-done.11
  41.6 0.6 %collective-permute-done.9 = bf16[2,128,128]{2,1,0:T(8,128)(2,1)S(1)} collective-permute-done((bf16[2,128,128]{2,1,0:T(8,128)(2,1)S(1)}, bf16[2,128,128]{2,1,0:T(8,128)(2,1)S(1)}, u32[]{:S(2)}, u32[]{:S(2)}) %collective-permute-start.9) | collective-permute-done | bytes 65568 | tf_op jit(solution)/shard_map/ppermute | solution.py:197
  42.2 2.5 %collective-permute-start.12 = (bf16[128,128]{1,0:T(8,128)(2,1)S(1)}, bf16[128,128]{1,0:T(8,128)(2,1)S(1)}, u32[]{:S(2)}, u32[]{:S(2)}) collective-permute-start(bf16[128,128]{1,0:T(8,128)(2,1)S(1)} %fusion.3), channel_id=1, source_target_pairs={{0,8},{2,10},{4,12},{6,14},{8,0},{10,2},{12,4},{14,6},{1,9},{3,11}... | collective-permute-start | bytes 98312 | tf_op jit(solution)/shard_map/ppermute | solution.py:197
  44.7 2.4 %collective-permute-done.12 = bf16[128,128]{1,0:T(8,128)(2,1)S(1)} collective-permute-done((bf16[128,128]{1,0:T(8,128)(2,1)S(1)}, bf16[128,128]{1,0:T(8,128)(2,1)S(1)}, u32[]{:S(2)}, u32[]{:S(2)}) %collective-permute-start.12) | collective-permute-done | bytes 32800 | tf_op jit(solution)/shard_map/ppermute | solution.py:197
  47.0 0.6 %fusion.2 = f32[128,128]{1,0:T(8,128)} fusion(f32[2,128,128]{2,1,0:T(8,128)S(1)} %fusion.1, bf16[128,128]{1,0:T(8,128)(2,1)S(1)} %collective-permute-done.12), kind=kLoop, calls=%fused_computation.5 | loop fusion | flops 32768 | bytes 163840 | tf_op jit(solution)/shard_map/add | solution.py:218
  (8 shorter events, 0.1 us)
Async XLA Ops:
  0.0 1.6 %copy-start = (bf16[128,16,512]{2,1,0:T(8,128)(2,1)S(1)}, bf16[128,16,512]{2,1,0:T(8,128)(2,1)}, u32[]{:S(2)}) copy-start(bf16[128,16,512]{2,1,0:T(8,128)(2,1)} %feats.1) | copy-start | bytes 6291460
  1.6 5.9 %copy-start.2 = (s32[128]{0:T(128)S(1)}, s32[128]{0:T(128)}, u32[]{:S(2)}) copy-start(s32[128]{0:T(128)} %param.5) | copy-start | bytes 1540
  1.6 22.7 %copy-start.1 = (bf16[512,4,512]{2,1,0:T(4,128)(2,1)S(1)}, bf16[512,4,512]{2,1,0:T(4,128)(2,1)}, u32[]{:S(2)}) copy-start(bf16[512,4,512]{2,1,0:T(4,128)(2,1)} %pool.1) | copy-start | bytes 6291460
  2.1 10.9 %collective-permute-start.2 = (bf16[520,128]{1,0:T(8,128)(2,1)S(1)}, bf16[520,128]{1,0:T(8,128)(2,1)S(1)}, u32[]{:S(2)}, u32[]{:S(2)}) collective-permute-start(bf16[520,128]{1,0:T(8,128)(2,1)S(1)} %get-tuple-element.20), channel_id=1, source_target_pairs={{0,12},{2,14},{4,8},{6,10},{8,4},{10,6},{12,0},{14,2},{1,13},{3,15... | collective-permute-start | bytes 399368 | tf_op jit(solution)/shard_map/ppermute | solution.py:197
  7.2 17.0 %collective-permute-start.3 = (bf16[520,128]{1,0:T(8,128)(2,1)S(1)}, bf16[520,128]{1,0:T(8,128)(2,1)S(1)}, u32[]{:S(2)}, u32[]{:S(2)}) collective-permute-start(bf16[520,128]{1,0:T(8,128)(2,1)S(1)} %get-tuple-element.21), channel_id=1, source_target_pairs={{0,10},{2,8},{4,14},{6,12},{8,2},{10,0},{12,6},{14,4},{1,11},{3,9}... | collective-permute-start | bytes 399368 | tf_op jit(solution)/shard_map/ppermute | solution.py:197
  7.5 5.0 %collective-permute-start.7 = (s32[128]{0:T(128)S(1)}, s32[128]{0:T(128)S(1)}, u32[]{:S(2)}, u32[]{:S(2)}) collective-permute-start(s32[128]{0:T(128)S(1)} %copy-done.2), channel_id=1, source_target_pairs={{0,1},{1,0},{2,3},{3,2},{4,5},{5,4},{6,7},{7,6},{8,9},{9,8},{10,11... | collective-permute-start | bytes 1544 | tf_op jit(solution)/shard_map/ppermute | solution.py:197
  7.5 17.5 %collective-permute-start.4 = (bf16[520,128]{1,0:T(8,128)(2,1)S(1)}, bf16[520,128]{1,0:T(8,128)(2,1)S(1)}, u32[]{:S(2)}, u32[]{:S(2)}) collective-permute-start(bf16[520,128]{1,0:T(8,128)(2,1)S(1)} %get-tuple-element.22), channel_id=1, source_target_pairs={{0,14},{2,12},{4,10},{6,8},{8,6},{10,4},{12,2},{14,0},{1,15},{3,13... | collective-permute-start | bytes 399368 | tf_op jit(solution)/shard_map/ppermute | solution.py:197
  10.0 15.1 %collective-permute-start.5 = (bf16[520,128]{1,0:T(8,128)(2,1)S(1)}, bf16[520,128]{1,0:T(8,128)(2,1)S(1)}, u32[]{:S(2)}, u32[]{:S(2)}) collective-permute-start(bf16[520,128]{1,0:T(8,128)(2,1)S(1)} %get-tuple-element.23), channel_id=1, source_target_pairs={{0,6},{2,4},{4,2},{6,0},{8,14},{10,12},{12,10},{14,8},{1,7},{3,5},... | collective-permute-start | bytes 399368 | tf_op jit(solution)/shard_map/ppermute | solution.py:197
  12.5 12.6 %collective-permute-start.6 = (bf16[520,128]{1,0:T(8,128)(2,1)S(1)}, bf16[520,128]{1,0:T(8,128)(2,1)S(1)}, u32[]{:S(2)}, u32[]{:S(2)}) collective-permute-start(bf16[520,128]{1,0:T(8,128)(2,1)S(1)} %get-tuple-element.24), channel_id=1, source_target_pairs={{0,4},{2,6},{4,0},{6,2},{8,12},{10,14},{12,8},{14,10},{1,5},{3,7},... | collective-permute-start | bytes 399368 | tf_op jit(solution)/shard_map/ppermute | solution.py:197
  13.0 16.9 %collective-permute-start = (bf16[520,128]{1,0:T(8,128)(2,1)S(1)}, bf16[520,128]{1,0:T(8,128)(2,1)S(1)}, u32[]{:S(2)}, u32[]{:S(2)}) collective-permute-start(bf16[520,128]{1,0:T(8,128)(2,1)S(1)} %get-tuple-element.18), channel_id=1, source_target_pairs={{0,8},{2,10},{4,12},{6,14},{8,0},{10,2},{12,4},{14,6},{1,9},{3,11}... | collective-permute-start | bytes 399368 | tf_op jit(solution)/shard_map/ppermute | solution.py:197
  24.2 5.6 %collective-permute-start.1 = (bf16[520,128]{1,0:T(8,128)(2,1)S(1)}, bf16[520,128]{1,0:T(8,128)(2,1)S(1)}, u32[]{:S(2)}, u32[]{:S(2)}) collective-permute-start(bf16[520,128]{1,0:T(8,128)(2,1)S(1)} %get-tuple-element.19), channel_id=1, source_target_pairs={{0,2},{2,0},{4,6},{6,4},{8,10},{10,8},{12,14},{14,12},{1,3},{3,1},... | collective-permute-start | bytes 399368 | tf_op jit(solution)/shard_map/ppermute | solution.py:197
  33.4 2.0 %collective-permute-start.8 = (f32[1024,128]{1,0:T(8,128)S(1)}, f32[1024,128]{1,0:T(8,128)S(1)}, u32[]{:S(2)}, u32[]{:S(2)}) collective-permute-start(f32[1024,128]{1,0:T(8,128)S(1)} %get-tuple-element.30), channel_id=1, source_target_pairs={{0,1},{1,0},{2,3},{3,2},{4,5},{5,4},{6,7},{7,6},{8,9},{9,8},{10,11... | collective-permute-start | bytes 1572872 | tf_op jit(solution)/shard_map/ppermute | solution.py:197
  35.6 5.5 %collective-permute-start.10 = (bf16[2,128,128]{2,1,0:T(8,128)(2,1)S(1)}, bf16[2,128,128]{2,1,0:T(8,128)(2,1)S(1)}, u32[]{:S(2)}, u32[]{:S(2)}) collective-permute-start(bf16[2,128,128]{2,1,0:T(8,128)(2,1)S(1)} %pad_maximum_fusion.1), channel_id=1, source_target_pairs={{0,6},{2,4},{4,2},{6,0},{8,14},{10,12},{12,10},{14,8},{1,7},{3,5},... | collective-permute-start | bytes 196616 | tf_op jit(solution)/shard_map/ppermute | solution.py:197
  36.2 5.3 %collective-permute-start.11 = (bf16[2,128,128]{2,1,0:T(8,128)(2,1)S(1)}, bf16[2,128,128]{2,1,0:T(8,128)(2,1)S(1)}, u32[]{:S(2)}, u32[]{:S(2)}) collective-permute-start(bf16[2,128,128]{2,1,0:T(8,128)(2,1)S(1)} %pad_maximum_fusion.2), channel_id=1, source_target_pairs={{0,2},{2,0},{4,6},{6,4},{8,10},{10,8},{12,14},{14,12},{1,3},{3,1},... | collective-permute-start | bytes 196616 | tf_op jit(solution)/shard_map/ppermute | solution.py:197
  37.5 4.6 %collective-permute-start.9 = (bf16[2,128,128]{2,1,0:T(8,128)(2,1)S(1)}, bf16[2,128,128]{2,1,0:T(8,128)(2,1)S(1)}, u32[]{:S(2)}, u32[]{:S(2)}) collective-permute-start(bf16[2,128,128]{2,1,0:T(8,128)(2,1)S(1)} %pad_maximum_fusion), channel_id=1, source_target_pairs={{0,4},{2,6},{4,0},{6,2},{8,12},{10,14},{12,8},{14,10},{1,5},{3,7},... | collective-permute-start | bytes 196616 | tf_op jit(solution)/shard_map/ppermute | solution.py:197
  42.2 4.9 %collective-permute-start.12 = (bf16[128,128]{1,0:T(8,128)(2,1)S(1)}, bf16[128,128]{1,0:T(8,128)(2,1)S(1)}, u32[]{:S(2)}, u32[]{:S(2)}) collective-permute-start(bf16[128,128]{1,0:T(8,128)(2,1)S(1)} %fusion.3), channel_id=1, source_target_pairs={{0,8},{2,10},{4,12},{6,14},{8,0},{10,2},{12,4},{14,6},{1,9},{3,11}... | collective-permute-start | bytes 98312 | tf_op jit(solution)/shard_map/ppermute | solution.py:197

commit v4 on v3

--- a/solution.py
+++ b/solution.py
@@ -15,7 +15,7 @@
 VMEM = pl.BlockSpec(memory_space=pltpu.VMEM)
 ORDER = (6, 5, 7, 4, 3, 2, 1, 0)
 LATE = (4, 1)
-NEAR = (2, 3, 1)
+NEAR = (3, 1, 2)
 PLAIN = ((1,), (0,))
 
 
@@ -165,15 +165,17 @@
     v = 2.0 * v.astype(F32) - inv * dot(v, high, PLAIN)
     b4 = 2.0 * b2 - dot(m2[0], m2[0], PLAIN)
     m4 = split(b4)
-    v = 2.0 * v - apply(v, m2)
+    b8 = 2.0 * b4 - dot(m4[0], m4[0], PLAIN)
+    m8 = split(b8)
+    vh = v.astype(BF16)
+    v = 2.0 * v - (dot(vh, m2[0], PLAIN) + dot(vh, m2[1], PLAIN))
     v = 2.0 * v - apply(v, m4)
-    w = v - apply(v, m4)
-    w = w - apply(w, m4)
-    precond = ((v + w) * inv).astype(BF16)
+    v = 2.0 * v - apply(v, m8)
+    precond = (v * inv).astype(BF16)
     half = precond.shape[0] // 2
     for rows, block in ((slice(0, ahead), early_feats[...]), (slice(ahead, count), f)):
         scores = dot(block, precond, ((1,), (1,)))
-        other[rows, :] = scores[:, half:]
+        other[rows, :] = scores[:, half:].astype(BF16)
         own[rows, :] = scores[:, :half]
 
 
@@ -182,9 +184,10 @@
     late_count = len(late) * (late[0].shape[0] - 8) * LANES // feat
     count = ahead[0].shape[0] + late_count
     half = jax.ShapeDtypeStruct((count, queries // 2), F32)
+    sent = jax.ShapeDtypeStruct(half.shape, BF16)
     return pl.pallas_call(
         functools.partial(score_kernel, modules),
-        out_shape=[half, half],
+        out_shape=[half, sent],
         in_specs=[VMEM] * (len(late) + 4),
         out_specs=[VMEM, VMEM],
         scratch_shapes=[pltpu.VMEM((late_count, feat), BF16)],
@@ -208,7 +211,7 @@
     first = [k for k in ORDER if k not in LATE]
     ahead = early([chunks[k] for k in first], feat)
     own, other = score([chunks[k] for k in LATE], ahead, picked, modules)
-    part = own + exchange(other, "pb", 1, 2)
+    part = own + exchange(other, "pb", 1, 2).astype(F32)
     part = part.reshape(peers, ex_dev, -1)
     place = {k: i for i, k in enumerate(first + list(LATE))}
     pair = lambda k: jnp.stack([part[place[k]], part[place[k + 4]]])

time: 47.8 us -> 47.1 us (0.985)
  no operation moved by 1% of the time
where the time goes in v4:
time: 47.1 us; the launch traced here: 47 us
  starting transfers between devices  25.1 us (53%)
  waiting for transfers between devices  14.2 us (30%)
  Pallas kernels  5.16 us (11%)
  local copies, waits for them, and re-layouts  1.63 us (3%)
  other arithmetic  0.77 us (2%)
    ppermute x13, starting transfers between devices, exchange(): return lax.ppermute(x, axes, [(i, i ^ k) for i in range(size)])  25.1 us
    ppermute x13, waiting for transfers between devices, exchange(): return lax.ppermute(x, axes, [(i, i ^ k) for i in range(size)])  14.2 us
    pallas_call x1, Pallas kernels, score(): pl.pallas_call(functools.partial(score_kernel, modules), out_shape=[half,...  3.29 us
    unnamed x6, local copies, waits for them, and re-layouts  1.6 us
  transfers between devices with their start and end apart: 13, of which 7 were waited for; matrix products, arithmetic and copies ran while one was open for 0% of the time, Pallas kernels for 3%

profile of v4, /device:TPU:0, one launch (start us, length us, event | category | flops | bytes accessed | tf_op | source)
XLA Modules:
  0.0 47.0 jit_solution(4074899732508618532)
XLA Ops:
  0.0 0.0 copy-start
  0.0 1.6 %copy-done = bf16[128,16,512]{2,1,0:T(8,128)(2,1)S(1)} copy-done((bf16[128,16,512]{2,1,0:T(8,128)(2,1)S(1)}, bf16[128,16,512]{2,1,0:T(8,128)(2,1)}, u32[]{:S(2)}) %copy-start) | copy-done | bytes 2097176
  1.6 0.0 copy-start.2
  1.6 0.0 copy-start.1
  1.6 0.5 pack.1
  2.1 5.1 %collective-permute-start.2 = (bf16[520,128]{1,0:T(8,128)(2,1)S(1)}, bf16[520,128]{1,0:T(8,128)(2,1)S(1)}, u32[]{:S(2)}, u32[]{:S(2)}) collective-permute-start(bf16[520,128]{1,0:T(8,128)(2,1)S(1)} %get-tuple-element.20), channel_id=1, source_target_pairs={{0,12},{2,14},{4,8},{6,10},{8,4},{10,6},{12,0},{14,2},{1,13},{3,15... | collective-permute-start | bytes 399368 | tf_op jit(solution)/shard_map/ppermute | solution.py:200
  7.2 0.4 collective-permute-start.3
  7.5 0.0 copy-done.2
  7.5 0.0 collective-permute-start.7
  7.5 2.4 %collective-permute-start.4 = (bf16[520,128]{1,0:T(8,128)(2,1)S(1)}, bf16[520,128]{1,0:T(8,128)(2,1)S(1)}, u32[]{:S(2)}, u32[]{:S(2)}) collective-permute-start(bf16[520,128]{1,0:T(8,128)(2,1)S(1)} %get-tuple-element.22), channel_id=1, source_target_pairs={{0,14},{2,12},{4,10},{6,8},{8,6},{10,4},{12,2},{14,0},{1,15},{3,13... | collective-permute-start | bytes 399368 | tf_op jit(solution)/shard_map/ppermute | solution.py:200
  10.0 2.5 %collective-permute-start.5 = (bf16[520,128]{1,0:T(8,128)(2,1)S(1)}, bf16[520,128]{1,0:T(8,128)(2,1)S(1)}, u32[]{:S(2)}, u32[]{:S(2)}) collective-permute-start(bf16[520,128]{1,0:T(8,128)(2,1)S(1)} %get-tuple-element.23), channel_id=1, source_target_pairs={{0,6},{2,4},{4,2},{6,0},{8,14},{10,12},{12,10},{14,8},{1,7},{3,5},... | collective-permute-start | bytes 399368 | tf_op jit(solution)/shard_map/ppermute | solution.py:200
  12.5 0.0 collective-permute-done.7
  12.5 0.5 collective-permute-start.6
  12.9 0.0 collective-permute-done.2.refs_0_
  13.0 7.9 %collective-permute-start = (bf16[520,128]{1,0:T(8,128)(2,1)S(1)}, bf16[520,128]{1,0:T(8,128)(2,1)S(1)}, u32[]{:S(2)}, u32[]{:S(2)}) collective-permute-start(bf16[520,128]{1,0:T(8,128)(2,1)S(1)} %get-tuple-element.18), channel_id=1, source_target_pairs={{0,8},{2,10},{4,12},{6,14},{8,0},{10,2},{12,4},{14,6},{1,9},{3,11}... | collective-permute-start | bytes 399368 | tf_op jit(solution)/shard_map/ppermute | solution.py:200
  20.9 3.3 %collective-permute-done.3.refs_1_ = bf16[520,128]{1,0:T(8,128)(2,1)S(1)} collective-permute-done((bf16[520,128]{1,0:T(8,128)(2,1)S(1)}, bf16[520,128]{1,0:T(8,128)(2,1)S(1)}, u32[]{:S(2)}, u32[]{:S(2)}) %collective-permute-start.3) | collective-permute-done | bytes 133152 | tf_op jit(solution)/shard_map/ppermute | solution.py:200
  24.2 0.0 collective-permute-start.1
  24.3 0.0 copy-done.1
  24.3 0.8 %pick.1.refs_5_ = bf16[256,512]{1,0:T(8,128)(2,1)S(1)} custom-call(bf16[512,4,512]{2,1,0:T(4,128)(2,1)S(1)} %copy-done.1, s32[1,256]{1,0:T(1,128)S(1)} %bitcast.23), custom_call_target="tpu_custom_call" | custom-call | tf_op jit(solution)/shard_map/pick/pallas_call | solution.py:94
  25.0 0.0 collective-permute-done.4.refs_2_
  25.0 0.0 collective-permute-done.5.refs_3_
  25.1 0.0 collective-permute-done.6.refs_4_
  25.1 0.7 %early.1 = (bf16[768,512]{1,0:T(8,128)(2,1)S(1)}, f32[512,512]{1,0:T(8,128)S(1)}, f32[8,128]{1,0:T(8,128)S(1)}) custom-call(bf16[520,128]{1,0:T(8,128)(2,1)S(1)} %collective-permute-done.2.refs_0_, bf16[520,128]{1,0:T(8,128)(2,1)S(1)} %collective-permute-done.3.refs_1_, bf16[520,128]{1,0:T(8,128)(2,1)S(1)} %collective-permute-done.4.refs_2_, ...), custom_call_target="tpu_custom_call" | custom-call | flops 402653184 | bytes 4194304 | tf_op jit(solution)/shard_map/early/pallas_call | solution.py:128
  25.7 4.1 %collective-permute-done.refs_0_ = bf16[520,128]{1,0:T(8,128)(2,1)S(1)} collective-permute-done((bf16[520,128]{1,0:T(8,128)(2,1)S(1)}, bf16[520,128]{1,0:T(8,128)(2,1)S(1)}, u32[]{:S(2)}, u32[]{:S(2)}) %collective-permute-start) | collective-permute-done | bytes 133152 | tf_op jit(solution)/shard_map/ppermute | solution.py:200
  29.8 0.0 collective-permute-done.1.refs_1_
  29.8 3.3 %score.1 = (f32[1024,128]{1,0:T(8,128)S(1)}, bf16[1024,128]{1,0:T(8,128)(2,1)S(1)}) custom-call(bf16[520,128]{1,0:T(8,128)(2,1)S(1)} %collective-permute-done.refs_0_, bf16[520,128]{1,0:T(8,128)(2,1)S(1)} %collective-permute-done.1.refs_1_, bf16[768,512]{1,0:T(8,128)(2,1)S(1)} %get-tuple-element.26.refs_2_, f32[512,512]{1,0:T(8,128)S(1)} %get-tuple-element.27.refs_3_, ...), custom_call_target="tpu_custom_call" | custom-call | tf_op jit(solution)/shard_map/score/pallas_call | solution.py:188
  33.1 0.1 collective-permute-start.8
  33.2 1.5 %collective-permute-done.8 = bf16[1024,128]{1,0:T(8,128)(2,1)S(1)} collective-permute-done((bf16[1024,128]{1,0:T(8,128)(2,1)S(1)}, bf16[1024,128]{1,0:T(8,128)(2,1)S(1)}, u32[]{:S(2)}, u32[]{:S(2)}) %collective-permute-start.8) | collective-permute-done | bytes 262176 | tf_op jit(solution)/shard_map/ppermute | solution.py:200
  34.7 0.1 fusion.4
  34.9 0.6 %collective-permute-start.9 = (bf16[2,128,128]{2,1,0:T(8,128)(2,1)S(1)}, bf16[2,128,128]{2,1,0:T(8,128)(2,1)S(1)}, u32[]{:S(2)}, u32[]{:S(2)}) collective-permute-start(bf16[2,128,128]{2,1,0:T(8,128)(2,1)S(1)} %pad_maximum_fusion), channel_id=1, source_target_pairs={{0,6},{2,4},{4,2},{6,0},{8,14},{10,12},{12,10},{14,8},{1,7},{3,5},... | collective-permute-start | bytes 196616 | tf_op jit(solution)/shard_map/ppermute | solution.py:200
  35.5 1.2 %collective-permute-start.10 = (bf16[2,128,128]{2,1,0:T(8,128)(2,1)S(1)}, bf16[2,128,128]{2,1,0:T(8,128)(2,1)S(1)}, u32[]{:S(2)}, u32[]{:S(2)}) collective-permute-start(bf16[2,128,128]{2,1,0:T(8,128)(2,1)S(1)} %pad_maximum_fusion.1), channel_id=1, source_target_pairs={{0,2},{2,0},{4,6},{6,4},{8,10},{10,8},{12,14},{14,12},{1,3},{3,1},... | collective-permute-start | bytes 196616 | tf_op jit(solution)/shard_map/ppermute | solution.py:200
  36.7 1.8 %collective-permute-start.11 = (bf16[2,128,128]{2,1,0:T(8,128)(2,1)S(1)}, bf16[2,128,128]{2,1,0:T(8,128)(2,1)S(1)}, u32[]{:S(2)}, u32[]{:S(2)}) collective-permute-start(bf16[2,128,128]{2,1,0:T(8,128)(2,1)S(1)} %pad_maximum_fusion.2), channel_id=1, source_target_pairs={{0,4},{2,6},{4,0},{6,2},{8,12},{10,14},{12,8},{14,10},{1,5},{3,7},... | collective-permute-start | bytes 196616 | tf_op jit(solution)/shard_map/ppermute | solution.py:200
  38.6 1.8 %collective-permute-done.9 = bf16[2,128,128]{2,1,0:T(8,128)(2,1)S(1)} collective-permute-done((bf16[2,128,128]{2,1,0:T(8,128)(2,1)S(1)}, bf16[2,128,128]{2,1,0:T(8,128)(2,1)S(1)}, u32[]{:S(2)}, u32[]{:S(2)}) %collective-permute-start.9) | collective-permute-done | bytes 65568 | tf_op jit(solution)/shard_map/ppermute | solution.py:200
  40.3 0.5 %collective-permute-done.10 = bf16[2,128,128]{2,1,0:T(8,128)(2,1)S(1)} collective-permute-done((bf16[2,128,128]{2,1,0:T(8,128)(2,1)S(1)}, bf16[2,128,128]{2,1,0:T(8,128)(2,1)S(1)}, u32[]{:S(2)}, u32[]{:S(2)}) %collective-permute-start.10) | collective-permute-done | bytes 65568 | tf_op jit(solution)/shard_map/ppermute | solution.py:200
  40.8 0.6 %collective-permute-done.11 = bf16[2,128,128]{2,1,0:T(8,128)(2,1)S(1)} collective-permute-done((bf16[2,128,128]{2,1,0:T(8,128)(2,1)S(1)}, bf16[2,128,128]{2,1,0:T(8,128)(2,1)S(1)}, u32[]{:S(2)}, u32[]{:S(2)}) %collective-permute-start.11) | collective-permute-done | bytes 65568 | tf_op jit(solution)/shard_map/ppermute | solution.py:200
  41.4 2.5 %collective-permute-start.12 = (bf16[128,128]{1,0:T(8,128)(2,1)S(1)}, bf16[128,128]{1,0:T(8,128)(2,1)S(1)}, u32[]{:S(2)}, u32[]{:S(2)}) collective-permute-start(bf16[128,128]{1,0:T(8,128)(2,1)S(1)} %fusion.3), channel_id=1, source_target_pairs={{0,8},{2,10},{4,12},{6,14},{8,0},{10,2},{12,4},{14,6},{1,9},{3,11}... | collective-permute-start | bytes 98312 | tf_op jit(solution)/shard_map/ppermute | solution.py:200
  43.9 2.4 %collective-permute-done.12 = bf16[128,128]{1,0:T(8,128)(2,1)S(1)} collective-permute-done((bf16[128,128]{1,0:T(8,128)(2,1)S(1)}, bf16[128,128]{1,0:T(8,128)(2,1)S(1)}, u32[]{:S(2)}, u32[]{:S(2)}) %collective-permute-start.12) | collective-permute-done | bytes 32800 | tf_op jit(solution)/shard_map/ppermute | solution.py:200
  46.3 0.6 %fusion.2 = f32[128,128]{1,0:T(8,128)} fusion(f32[2,128,128]{2,1,0:T(8,128)S(1)} %fusion.1, bf16[128,128]{1,0:T(8,128)(2,1)S(1)} %collective-permute-done.12), kind=kLoop, calls=%fused_computation.6 | loop fusion | flops 32768 | bytes 163840 | tf_op jit(solution)/shard_map/add | solution.py:221
  (8 shorter events, 0.1 us)
Async XLA Ops:
  0.0 1.6 %copy-start = (bf16[128,16,512]{2,1,0:T(8,128)(2,1)S(1)}, bf16[128,16,512]{2,1,0:T(8,128)(2,1)}, u32[]{:S(2)}) copy-start(bf16[128,16,512]{2,1,0:T(8,128)(2,1)} %feats.1) | copy-start | bytes 6291460
  1.6 5.9 %copy-start.2 = (s32[128]{0:T(128)S(1)}, s32[128]{0:T(128)}, u32[]{:S(2)}) copy-start(s32[128]{0:T(128)} %param.5) | copy-start | bytes 1540
  1.6 22.7 %copy-start.1 = (bf16[512,4,512]{2,1,0:T(4,128)(2,1)S(1)}, bf16[512,4,512]{2,1,0:T(4,128)(2,1)}, u32[]{:S(2)}) copy-start(bf16[512,4,512]{2,1,0:T(4,128)(2,1)} %pool.1) | copy-start | bytes 6291460
  2.1 10.9 %collective-permute-start.2 = (bf16[520,128]{1,0:T(8,128)(2,1)S(1)}, bf16[520,128]{1,0:T(8,128)(2,1)S(1)}, u32[]{:S(2)}, u32[]{:S(2)}) collective-permute-start(bf16[520,128]{1,0:T(8,128)(2,1)S(1)} %get-tuple-element.20), channel_id=1, source_target_pairs={{0,12},{2,14},{4,8},{6,10},{8,4},{10,6},{12,0},{14,2},{1,13},{3,15... | collective-permute-start | bytes 399368 | tf_op jit(solution)/shard_map/ppermute | solution.py:200
  7.2 17.0 %collective-permute-start.3 = (bf16[520,128]{1,0:T(8,128)(2,1)S(1)}, bf16[520,128]{1,0:T(8,128)(2,1)S(1)}, u32[]{:S(2)}, u32[]{:S(2)}) collective-permute-start(bf16[520,128]{1,0:T(8,128)(2,1)S(1)} %get-tuple-element.21), channel_id=1, source_target_pairs={{0,10},{2,8},{4,14},{6,12},{8,2},{10,0},{12,6},{14,4},{1,11},{3,9}... | collective-permute-start | bytes 399368 | tf_op jit(solution)/shard_map/ppermute | solution.py:200
  7.5 5.0 %collective-permute-start.7 = (s32[128]{0:T(128)S(1)}, s32[128]{0:T(128)S(1)}, u32[]{:S(2)}, u32[]{:S(2)}) collective-permute-start(s32[128]{0:T(128)S(1)} %copy-done.2), channel_id=1, source_target_pairs={{0,1},{1,0},{2,3},{3,2},{4,5},{5,4},{6,7},{7,6},{8,9},{9,8},{10,11... | collective-permute-start | bytes 1544 | tf_op jit(solution)/shard_map/ppermute | solution.py:200
  7.5 17.5 %collective-permute-start.4 = (bf16[520,128]{1,0:T(8,128)(2,1)S(1)}, bf16[520,128]{1,0:T(8,128)(2,1)S(1)}, u32[]{:S(2)}, u32[]{:S(2)}) collective-permute-start(bf16[520,128]{1,0:T(8,128)(2,1)S(1)} %get-tuple-element.22), channel_id=1, source_target_pairs={{0,14},{2,12},{4,10},{6,8},{8,6},{10,4},{12,2},{14,0},{1,15},{3,13... | collective-permute-start | bytes 399368 | tf_op jit(solution)/shard_map/ppermute | solution.py:200
  10.0 15.1 %collective-permute-start.5 = (bf16[520,128]{1,0:T(8,128)(2,1)S(1)}, bf16[520,128]{1,0:T(8,128)(2,1)S(1)}, u32[]{:S(2)}, u32[]{:S(2)}) collective-permute-start(bf16[520,128]{1,0:T(8,128)(2,1)S(1)} %get-tuple-element.23), channel_id=1, source_target_pairs={{0,6},{2,4},{4,2},{6,0},{8,14},{10,12},{12,10},{14,8},{1,7},{3,5},... | collective-permute-start | bytes 399368 | tf_op jit(solution)/shard_map/ppermute | solution.py:200
  12.5 12.6 %collective-permute-start.6 = (bf16[520,128]{1,0:T(8,128)(2,1)S(1)}, bf16[520,128]{1,0:T(8,128)(2,1)S(1)}, u32[]{:S(2)}, u32[]{:S(2)}) collective-permute-start(bf16[520,128]{1,0:T(8,128)(2,1)S(1)} %get-tuple-element.24), channel_id=1, source_target_pairs={{0,4},{2,6},{4,0},{6,2},{8,12},{10,14},{12,8},{14,10},{1,5},{3,7},... | collective-permute-start | bytes 399368 | tf_op jit(solution)/shard_map/ppermute | solution.py:200
  13.0 16.9 %collective-permute-start = (bf16[520,128]{1,0:T(8,128)(2,1)S(1)}, bf16[520,128]{1,0:T(8,128)(2,1)S(1)}, u32[]{:S(2)}, u32[]{:S(2)}) collective-permute-start(bf16[520,128]{1,0:T(8,128)(2,1)S(1)} %get-tuple-element.18), channel_id=1, source_target_pairs={{0,8},{2,10},{4,12},{6,14},{8,0},{10,2},{12,4},{14,6},{1,9},{3,11}... | collective-permute-start | bytes 399368 | tf_op jit(solution)/shard_map/ppermute | solution.py:200
  24.2 5.6 %collective-permute-start.1 = (bf16[520,128]{1,0:T(8,128)(2,1)S(1)}, bf16[520,128]{1,0:T(8,128)(2,1)S(1)}, u32[]{:S(2)}, u32[]{:S(2)}) collective-permute-start(bf16[520,128]{1,0:T(8,128)(2,1)S(1)} %get-tuple-element.19), channel_id=1, source_target_pairs={{0,2},{2,0},{4,6},{6,4},{8,10},{10,8},{12,14},{14,12},{1,3},{3,1},... | collective-permute-start | bytes 399368 | tf_op jit(solution)/shard_map/ppermute | solution.py:200
  33.1 1.6 %collective-permute-start.8 = (bf16[1024,128]{1,0:T(8,128)(2,1)S(1)}, bf16[1024,128]{1,0:T(8,128)(2,1)S(1)}, u32[]{:S(2)}, u32[]{:S(2)}) collective-permute-start(bf16[1024,128]{1,0:T(8,128)(2,1)S(1)} %get-tuple-element.30), channel_id=1, source_target_pairs={{0,1},{1,0},{2,3},{3,2},{4,5},{5,4},{6,7},{7,6},{8,9},{9,8},{10,11... | collective-permute-start | bytes 786440 | tf_op jit(solution)/shard_map/ppermute | solution.py:200
  34.9 5.5 %collective-permute-start.9 = (bf16[2,128,128]{2,1,0:T(8,128)(2,1)S(1)}, bf16[2,128,128]{2,1,0:T(8,128)(2,1)S(1)}, u32[]{:S(2)}, u32[]{:S(2)}) collective-permute-start(bf16[2,128,128]{2,1,0:T(8,128)(2,1)S(1)} %pad_maximum_fusion), channel_id=1, source_target_pairs={{0,6},{2,4},{4,2},{6,0},{8,14},{10,12},{12,10},{14,8},{1,7},{3,5},... | collective-permute-start | bytes 196616 | tf_op jit(solution)/shard_map/ppermute | solution.py:200
  35.5 5.3 %collective-permute-start.10 = (bf16[2,128,128]{2,1,0:T(8,128)(2,1)S(1)}, bf16[2,128,128]{2,1,0:T(8,128)(2,1)S(1)}, u32[]{:S(2)}, u32[]{:S(2)}) collective-permute-start(bf16[2,128,128]{2,1,0:T(8,128)(2,1)S(1)} %pad_maximum_fusion.1), channel_id=1, source_target_pairs={{0,2},{2,0},{4,6},{6,4},{8,10},{10,8},{12,14},{14,12},{1,3},{3,1},... | collective-permute-start | bytes 196616 | tf_op jit(solution)/shard_map/ppermute | solution.py:200
  36.7 4.6 %collective-permute-start.11 = (bf16[2,128,128]{2,1,0:T(8,128)(2,1)S(1)}, bf16[2,128,128]{2,1,0:T(8,128)(2,1)S(1)}, u32[]{:S(2)}, u32[]{:S(2)}) collective-permute-start(bf16[2,128,128]{2,1,0:T(8,128)(2,1)S(1)} %pad_maximum_fusion.2), channel_id=1, source_target_pairs={{0,4},{2,6},{4,0},{6,2},{8,12},{10,14},{12,8},{14,10},{1,5},{3,7},... | collective-permute-start | bytes 196616 | tf_op jit(solution)/shard_map/ppermute | solution.py:200
  41.4 4.9 %collective-permute-start.12 = (bf16[128,128]{1,0:T(8,128)(2,1)S(1)}, bf16[128,128]{1,0:T(8,128)(2,1)S(1)}, u32[]{:S(2)}, u32[]{:S(2)}) collective-permute-start(bf16[128,128]{1,0:T(8,128)(2,1)S(1)} %fusion.3), channel_id=1, source_target_pairs={{0,8},{2,10},{4,12},{6,14},{8,0},{10,2},{12,4},{14,6},{1,9},{3,11}... | collective-permute-start | bytes 98312 | tf_op jit(solution)/shard_map/ppermute | solution.py:200

commit v5 on v4

--- a/solution.py
+++ b/solution.py
@@ -13,9 +13,10 @@
 LANES = 128
 GROUP = ("gx", "row")
 VMEM = pl.BlockSpec(memory_space=pltpu.VMEM)
-ORDER = (6, 5, 7, 4, 3, 2, 1, 0)
+ORDER = (6, 1, 5, 7, 4, 3, 2, 0)
 LATE = (4, 1)
-NEAR = (3, 1, 2)
+AHEAD = tuple(k for k in ORDER if k not in LATE)
+NEAR = (2, 3, 1)
 PLAIN = ((1,), (0,))
 
 
@@ -173,21 +174,22 @@
     v = 2.0 * v - apply(v, m8)
     precond = (v * inv).astype(BF16)
     half = precond.shape[0] // 2
-    for rows, block in ((slice(0, ahead), early_feats[...]), (slice(ahead, count), f)):
+    ex_dev = feats.shape[0] // len(LATE)
+    for keys, block in ((AHEAD, early_feats[...]), (LATE, f)):
         scores = dot(block, precond, ((1,), (1,)))
-        other[rows, :] = scores[:, half:].astype(BF16)
-        own[rows, :] = scores[:, :half]
+        for i, k in enumerate(keys):
+            rows = scores[i * ex_dev : (i + 1) * ex_dev]
+            other[k % 4, k // 4] = rows[:, half:].astype(BF16)
+            own[k % 4, k // 4] = rows[:, :half]
 
 
 def score(late, ahead, picked, modules):
     queries, feat = picked.shape
     late_count = len(late) * (late[0].shape[0] - 8) * LANES // feat
-    count = ahead[0].shape[0] + late_count
-    half = jax.ShapeDtypeStruct((count, queries // 2), F32)
-    sent = jax.ShapeDtypeStruct(half.shape, BF16)
+    block = (4, 2, late_count // len(late), queries // 2)
     return pl.pallas_call(
         functools.partial(score_kernel, modules),
-        out_shape=[half, sent],
+        out_shape=[jax.ShapeDtypeStruct(block, F32), jax.ShapeDtypeStruct(block, BF16)],
         in_specs=[VMEM] * (len(late) + 4),
         out_specs=[VMEM, VMEM],
         scratch_shapes=[pltpu.VMEM((late_count, feat), BF16)],
@@ -208,16 +210,12 @@
     for k in ORDER[:-1]:
         chunks[k] = exchange(chunks[k], GROUP, k, peers)
     picked = pick(query_pool, ids)
-    first = [k for k in ORDER if k not in LATE]
-    ahead = early([chunks[k] for k in first], feat)
+    ahead = early([chunks[k] for k in AHEAD], feat)
     own, other = score([chunks[k] for k in LATE], ahead, picked, modules)
     part = own + exchange(other, "pb", 1, 2).astype(F32)
-    part = part.reshape(peers, ex_dev, -1)
-    place = {k: i for i, k in enumerate(first + list(LATE))}
-    pair = lambda k: jnp.stack([part[place[k]], part[place[k + 4]]])
-    near = pair(0)
+    near = part[0]
     for k in NEAR:
-        near = near + exchange(pair(k).astype(BF16), GROUP, k, peers).astype(F32)
+        near = near + exchange(part[k].astype(BF16), GROUP, k, peers).astype(F32)
     return near[0] + exchange(near[1].astype(BF16), GROUP, 4, peers).astype(F32)
 
 

time: 47.1 us -> 47.1 us (level)
  no operation moved by 1% of the time
where the time goes in v5:
time: 47.1 us; the launch traced here: 46.9 us
  starting transfers between devices  24.8 us (53%)
  waiting for transfers between devices  14.5 us (31%)
  Pallas kernels  5.16 us (11%)
  local copies, waits for them, and re-layouts  1.62 us (3%)
  other arithmetic  0.76 us (2%)
    ppermute x13, starting transfers between devices, exchange(): return lax.ppermute(x, axes, [(i, i ^ k) for i in range(size)])  24.8 us
    ppermute x13, waiting for transfers between devices, exchange(): return lax.ppermute(x, axes, [(i, i ^ k) for i in range(size)])  14.5 us
    pallas_call x1, Pallas kernels, score(): pl.pallas_call(functools.partial(score_kernel, modules), out_shape=[jax.S...  3.29 us
    unnamed x6, local copies, waits for them, and re-layouts  1.6 us
  transfers between devices with their start and end apart: 13, of which 7 were waited for; matrix products, arithmetic and copies ran while one was open for 0% of the time, Pallas kernels for 3%

profile of v5, /device:TPU:0, one launch (start us, length us, event | category | flops | bytes accessed | tf_op | source)
XLA Modules:
  0.0 46.9 jit_solution(11014636868120845389)
XLA Ops:
  0.0 0.0 copy-start
  0.0 1.6 %copy-done = bf16[128,16,512]{2,1,0:T(8,128)(2,1)S(1)} copy-done((bf16[128,16,512]{2,1,0:T(8,128)(2,1)S(1)}, bf16[128,16,512]{2,1,0:T(8,128)(2,1)}, u32[]{:S(2)}) %copy-start) | copy-done | bytes 2097176
  1.6 0.0 copy-start.2
  1.6 0.0 copy-start.1
  1.6 0.5 pack.1
  2.1 5.1 %collective-permute-start.2 = (bf16[520,128]{1,0:T(8,128)(2,1)S(1)}, bf16[520,128]{1,0:T(8,128)(2,1)S(1)}, u32[]{:S(2)}, u32[]{:S(2)}) collective-permute-start(bf16[520,128]{1,0:T(8,128)(2,1)S(1)} %get-tuple-element.20), channel_id=1, source_target_pairs={{0,12},{2,14},{4,8},{6,10},{8,4},{10,6},{12,0},{14,2},{1,13},{3,15... | collective-permute-start | bytes 399368 | tf_op jit(solution)/shard_map/ppermute | solution.py:202
  7.2 0.4 collective-permute-start.3
  7.5 0.0 copy-done.2
  7.5 0.0 collective-permute-start.7
  7.5 2.4 %collective-permute-start.4 = (bf16[520,128]{1,0:T(8,128)(2,1)S(1)}, bf16[520,128]{1,0:T(8,128)(2,1)S(1)}, u32[]{:S(2)}, u32[]{:S(2)}) collective-permute-start(bf16[520,128]{1,0:T(8,128)(2,1)S(1)} %get-tuple-element.22), channel_id=1, source_target_pairs={{0,14},{2,12},{4,10},{6,8},{8,6},{10,4},{12,2},{14,0},{1,15},{3,13... | collective-permute-start | bytes 399368 | tf_op jit(solution)/shard_map/ppermute | solution.py:202
  10.0 2.5 %collective-permute-start.5 = (bf16[520,128]{1,0:T(8,128)(2,1)S(1)}, bf16[520,128]{1,0:T(8,128)(2,1)S(1)}, u32[]{:S(2)}, u32[]{:S(2)}) collective-permute-start(bf16[520,128]{1,0:T(8,128)(2,1)S(1)} %get-tuple-element.23), channel_id=1, source_target_pairs={{0,6},{2,4},{4,2},{6,0},{8,14},{10,12},{12,10},{14,8},{1,7},{3,5},... | collective-permute-start | bytes 399368 | tf_op jit(solution)/shard_map/ppermute | solution.py:202
  12.5 0.0 collective-permute-done.7
  12.5 0.5 collective-permute-start.6
  12.9 0.0 collective-permute-done.2.refs_0_
  13.0 7.9 %collective-permute-start = (bf16[520,128]{1,0:T(8,128)(2,1)S(1)}, bf16[520,128]{1,0:T(8,128)(2,1)S(1)}, u32[]{:S(2)}, u32[]{:S(2)}) collective-permute-start(bf16[520,128]{1,0:T(8,128)(2,1)S(1)} %get-tuple-element.18), channel_id=1, source_target_pairs={{0,8},{2,10},{4,12},{6,14},{8,0},{10,2},{12,4},{14,6},{1,9},{3,11}... | collective-permute-start | bytes 399368 | tf_op jit(solution)/shard_map/ppermute | solution.py:202
  20.9 3.3 %collective-permute-done.3.refs_1_ = bf16[520,128]{1,0:T(8,128)(2,1)S(1)} collective-permute-done((bf16[520,128]{1,0:T(8,128)(2,1)S(1)}, bf16[520,128]{1,0:T(8,128)(2,1)S(1)}, u32[]{:S(2)}, u32[]{:S(2)}) %collective-permute-start.3) | collective-permute-done | bytes 133152 | tf_op jit(solution)/shard_map/ppermute | solution.py:202
  24.2 0.0 collective-permute-start.1
  24.3 0.0 copy-done.1
  24.3 0.8 %pick.1.refs_5_ = bf16[256,512]{1,0:T(8,128)(2,1)S(1)} custom-call(bf16[512,4,512]{2,1,0:T(4,128)(2,1)S(1)} %copy-done.1, s32[1,256]{1,0:T(1,128)S(1)} %bitcast.21), custom_call_target="tpu_custom_call" | custom-call | tf_op jit(solution)/shard_map/pick/pallas_call | solution.py:95
  25.0 0.0 collective-permute-done.4.refs_2_
  25.0 0.0 collective-permute-done.5.refs_3_
  25.1 0.0 collective-permute-done.6.refs_4_
  25.1 0.7 %early.1 = (bf16[768,512]{1,0:T(8,128)(2,1)S(1)}, f32[512,512]{1,0:T(8,128)S(1)}, f32[8,128]{1,0:T(8,128)S(1)}) custom-call(bf16[520,128]{1,0:T(8,128)(2,1)S(1)} %collective-permute-done.2.refs_0_, bf16[520,128]{1,0:T(8,128)(2,1)S(1)} %collective-permute-done.3.refs_1_, bf16[520,128]{1,0:T(8,128)(2,1)S(1)} %collective-permute-done.4.refs_2_, ...), custom_call_target="tpu_custom_call" | custom-call | flops 402653184 | bytes 4194304 | tf_op jit(solution)/shard_map/early/pallas_call | solution.py:129
  25.7 4.1 %collective-permute-done.refs_0_ = bf16[520,128]{1,0:T(8,128)(2,1)S(1)} collective-permute-done((bf16[520,128]{1,0:T(8,128)(2,1)S(1)}, bf16[520,128]{1,0:T(8,128)(2,1)S(1)}, u32[]{:S(2)}, u32[]{:S(2)}) %collective-permute-start) | collective-permute-done | bytes 133152 | tf_op jit(solution)/shard_map/ppermute | solution.py:202
  29.8 0.0 collective-permute-done.1.refs_1_
  29.8 3.3 %score.1 = (f32[4,2,128,128]{3,2,1,0:T(8,128)S(1)}, bf16[4,2,128,128]{3,2,1,0:T(8,128)(2,1)S(1)}) custom-call(bf16[520,128]{1,0:T(8,128)(2,1)S(1)} %collective-permute-done.refs_0_, bf16[520,128]{1,0:T(8,128)(2,1)S(1)} %collective-permute-done.1.refs_1_, bf16[768,512]{1,0:T(8,128)(2,1)S(1)} %get-tuple-element.26.refs_2_, ...), custom_call_target="tpu_custom_call" | custom-call | tf_op jit(solution)/shard_map/score/pallas_call | solution.py:190
  33.1 0.1 collective-permute-start.8
  33.2 1.5 %collective-permute-done.8 = bf16[4,2,128,128]{3,2,1,0:T(8,128)(2,1)S(1)} collective-permute-done((bf16[4,2,128,128]{3,2,1,0:T(8,128)(2,1)S(1)}, bf16[4,2,128,128]{3,2,1,0:T(8,128)(2,1)S(1)}, u32[]{:S(2)}, u32[]{:S(2)}) %collective-permute-start.8) | collective-permute-done | bytes 262176 | tf_op jit(solution)/shard_map/ppermute | solution.py:202
  34.7 0.1 fusion.5
  34.9 0.6 %collective-permute-start.10 = (bf16[2,128,128]{2,1,0:T(8,128)(2,1)S(1)}, bf16[2,128,128]{2,1,0:T(8,128)(2,1)S(1)}, u32[]{:S(2)}, u32[]{:S(2)}) collective-permute-start(bf16[2,128,128]{2,1,0:T(8,128)(2,1)S(1)} %get-tuple-element.35), channel_id=1, source_target_pairs={{0,6},{2,4},{4,2},{6,0},{8,14},{10,12},{12,10},{14,8},{1,7},{3,5},... | collective-permute-start | bytes 196616 | tf_op jit(solution)/shard_map/ppermute | solution.py:202
  35.5 1.2 %collective-permute-start.11 = (bf16[2,128,128]{2,1,0:T(8,128)(2,1)S(1)}, bf16[2,128,128]{2,1,0:T(8,128)(2,1)S(1)}, u32[]{:S(2)}, u32[]{:S(2)}) collective-permute-start(bf16[2,128,128]{2,1,0:T(8,128)(2,1)S(1)} %get-tuple-element.34), channel_id=1, source_target_pairs={{0,2},{2,0},{4,6},{6,4},{8,10},{10,8},{12,14},{14,12},{1,3},{3,1},... | collective-permute-start | bytes 196616 | tf_op jit(solution)/shard_map/ppermute | solution.py:202
  36.7 1.7 %collective-permute-start.9 = (bf16[2,128,128]{2,1,0:T(8,128)(2,1)S(1)}, bf16[2,128,128]{2,1,0:T(8,128)(2,1)S(1)}, u32[]{:S(2)}, u32[]{:S(2)}) collective-permute-start(bf16[2,128,128]{2,1,0:T(8,128)(2,1)S(1)} %get-tuple-element.33), channel_id=1, source_target_pairs={{0,4},{2,6},{4,0},{6,2},{8,12},{10,14},{12,8},{14,10},{1,5},{3,7},... | collective-permute-start | bytes 196616 | tf_op jit(solution)/shard_map/ppermute | solution.py:202
  38.4 2.1 %collective-permute-done.10 = bf16[2,128,128]{2,1,0:T(8,128)(2,1)S(1)} collective-permute-done((bf16[2,128,128]{2,1,0:T(8,128)(2,1)S(1)}, bf16[2,128,128]{2,1,0:T(8,128)(2,1)S(1)}, u32[]{:S(2)}, u32[]{:S(2)}) %collective-permute-start.10) | collective-permute-done | bytes 65568 | tf_op jit(solution)/shard_map/ppermute | solution.py:202
  40.5 0.3 collective-permute-done.11
  40.8 0.6 %collective-permute-done.9 = bf16[2,128,128]{2,1,0:T(8,128)(2,1)S(1)} collective-permute-done((bf16[2,128,128]{2,1,0:T(8,128)(2,1)S(1)}, bf16[2,128,128]{2,1,0:T(8,128)(2,1)S(1)}, u32[]{:S(2)}, u32[]{:S(2)}) %collective-permute-start.9) | collective-permute-done | bytes 65568 | tf_op jit(solution)/shard_map/ppermute | solution.py:202
  41.4 2.4 %collective-permute-start.12 = (bf16[128,128]{1,0:T(8,128)(2,1)S(1)}, bf16[128,128]{1,0:T(8,128)(2,1)S(1)}, u32[]{:S(2)}, u32[]{:S(2)}) collective-permute-start(bf16[128,128]{1,0:T(8,128)(2,1)S(1)} %fusion.4), channel_id=1, source_target_pairs={{0,8},{2,10},{4,12},{6,14},{8,0},{10,2},{12,4},{14,6},{1,9},{3,11}... | collective-permute-start | bytes 98312 | tf_op jit(solution)/shard_map/ppermute | solution.py:202
  43.8 2.5 %collective-permute-done.12 = bf16[128,128]{1,0:T(8,128)(2,1)S(1)} collective-permute-done((bf16[128,128]{1,0:T(8,128)(2,1)S(1)}, bf16[128,128]{1,0:T(8,128)(2,1)S(1)}, u32[]{:S(2)}, u32[]{:S(2)}) %collective-permute-start.12) | collective-permute-done | bytes 32800 | tf_op jit(solution)/shard_map/ppermute | solution.py:202
  46.3 0.6 %fusion.3 = f32[128,128]{1,0:T(8,128)} fusion(f32[2,128,128]{2,1,0:T(8,128)S(1)} %fusion.2, bf16[128,128]{1,0:T(8,128)(2,1)S(1)} %collective-permute-done.12), kind=kLoop, calls=%fused_computation.7 | loop fusion | flops 32768 | bytes 163840 | tf_op jit(solution)/shard_map/add | solution.py:219
  (4 shorter events, 0.1 us)
Async XLA Ops:
  0.0 1.6 %copy-start = (bf16[128,16,512]{2,1,0:T(8,128)(2,1)S(1)}, bf16[128,16,512]{2,1,0:T(8,128)(2,1)}, u32[]{:S(2)}) copy-start(bf16[128,16,512]{2,1,0:T(8,128)(2,1)} %feats.1) | copy-start | bytes 6291460
  1.6 5.9 %copy-start.2 = (s32[128]{0:T(128)S(1)}, s32[128]{0:T(128)}, u32[]{:S(2)}) copy-start(s32[128]{0:T(128)} %param.5) | copy-start | bytes 1540
  1.6 22.7 %copy-start.1 = (bf16[512,4,512]{2,1,0:T(4,128)(2,1)S(1)}, bf16[512,4,512]{2,1,0:T(4,128)(2,1)}, u32[]{:S(2)}) copy-start(bf16[512,4,512]{2,1,0:T(4,128)(2,1)} %pool.1) | copy-start | bytes 6291460
  2.1 10.9 %collective-permute-start.2 = (bf16[520,128]{1,0:T(8,128)(2,1)S(1)}, bf16[520,128]{1,0:T(8,128)(2,1)S(1)}, u32[]{:S(2)}, u32[]{:S(2)}) collective-permute-start(bf16[520,128]{1,0:T(8,128)(2,1)S(1)} %get-tuple-element.20), channel_id=1, source_target_pairs={{0,12},{2,14},{4,8},{6,10},{8,4},{10,6},{12,0},{14,2},{1,13},{3,15... | collective-permute-start | bytes 399368 | tf_op jit(solution)/shard_map/ppermute | solution.py:202
  7.2 17.0 %collective-permute-start.3 = (bf16[520,128]{1,0:T(8,128)(2,1)S(1)}, bf16[520,128]{1,0:T(8,128)(2,1)S(1)}, u32[]{:S(2)}, u32[]{:S(2)}) collective-permute-start(bf16[520,128]{1,0:T(8,128)(2,1)S(1)} %get-tuple-element.21), channel_id=1, source_target_pairs={{0,10},{2,8},{4,14},{6,12},{8,2},{10,0},{12,6},{14,4},{1,11},{3,9}... | collective-permute-start | bytes 399368 | tf_op jit(solution)/shard_map/ppermute | solution.py:202
  7.5 5.0 %collective-permute-start.7 = (s32[128]{0:T(128)S(1)}, s32[128]{0:T(128)S(1)}, u32[]{:S(2)}, u32[]{:S(2)}) collective-permute-start(s32[128]{0:T(128)S(1)} %copy-done.2), channel_id=1, source_target_pairs={{0,1},{1,0},{2,3},{3,2},{4,5},{5,4},{6,7},{7,6},{8,9},{9,8},{10,11... | collective-permute-start | bytes 1544 | tf_op jit(solution)/shard_map/ppermute | solution.py:202
  7.5 17.5 %collective-permute-start.4 = (bf16[520,128]{1,0:T(8,128)(2,1)S(1)}, bf16[520,128]{1,0:T(8,128)(2,1)S(1)}, u32[]{:S(2)}, u32[]{:S(2)}) collective-permute-start(bf16[520,128]{1,0:T(8,128)(2,1)S(1)} %get-tuple-element.22), channel_id=1, source_target_pairs={{0,14},{2,12},{4,10},{6,8},{8,6},{10,4},{12,2},{14,0},{1,15},{3,13... | collective-permute-start | bytes 399368 | tf_op jit(solution)/shard_map/ppermute | solution.py:202
  10.0 15.1 %collective-permute-start.5 = (bf16[520,128]{1,0:T(8,128)(2,1)S(1)}, bf16[520,128]{1,0:T(8,128)(2,1)S(1)}, u32[]{:S(2)}, u32[]{:S(2)}) collective-permute-start(bf16[520,128]{1,0:T(8,128)(2,1)S(1)} %get-tuple-element.23), channel_id=1, source_target_pairs={{0,6},{2,4},{4,2},{6,0},{8,14},{10,12},{12,10},{14,8},{1,7},{3,5},... | collective-permute-start | bytes 399368 | tf_op jit(solution)/shard_map/ppermute | solution.py:202
  12.5 12.6 %collective-permute-start.6 = (bf16[520,128]{1,0:T(8,128)(2,1)S(1)}, bf16[520,128]{1,0:T(8,128)(2,1)S(1)}, u32[]{:S(2)}, u32[]{:S(2)}) collective-permute-start(bf16[520,128]{1,0:T(8,128)(2,1)S(1)} %get-tuple-element.24), channel_id=1, source_target_pairs={{0,4},{2,6},{4,0},{6,2},{8,12},{10,14},{12,8},{14,10},{1,5},{3,7},... | collective-permute-start | bytes 399368 | tf_op jit(solution)/shard_map/ppermute | solution.py:202
  13.0 16.9 %collective-permute-start = (bf16[520,128]{1,0:T(8,128)(2,1)S(1)}, bf16[520,128]{1,0:T(8,128)(2,1)S(1)}, u32[]{:S(2)}, u32[]{:S(2)}) collective-permute-start(bf16[520,128]{1,0:T(8,128)(2,1)S(1)} %get-tuple-element.18), channel_id=1, source_target_pairs={{0,8},{2,10},{4,12},{6,14},{8,0},{10,2},{12,4},{14,6},{1,9},{3,11}... | collective-permute-start | bytes 399368 | tf_op jit(solution)/shard_map/ppermute | solution.py:202
  24.2 5.6 %collective-permute-start.1 = (bf16[520,128]{1,0:T(8,128)(2,1)S(1)}, bf16[520,128]{1,0:T(8,128)(2,1)S(1)}, u32[]{:S(2)}, u32[]{:S(2)}) collective-permute-start(bf16[520,128]{1,0:T(8,128)(2,1)S(1)} %get-tuple-element.19), channel_id=1, source_target_pairs={{0,2},{2,0},{4,6},{6,4},{8,10},{10,8},{12,14},{14,12},{1,3},{3,1},... | collective-permute-start | bytes 399368 | tf_op jit(solution)/shard_map/ppermute | solution.py:202
  33.1 1.6 %collective-permute-start.8 = (bf16[4,2,128,128]{3,2,1,0:T(8,128)(2,1)S(1)}, bf16[4,2,128,128]{3,2,1,0:T(8,128)(2,1)S(1)}, u32[]{:S(2)}, u32[]{:S(2)}) collective-permute-start(bf16[4,2,128,128]{3,2,1,0:T(8,128)(2,1)S(1)} %get-tuple-element.30), channel_id=1, source_target_pairs={{0,1},{1,0},{2,3},{3,2},{4,5},{5,4},{6,7},{7,6},{8,9},{9,8},{10,11... | collective-permute-start | bytes 786440 | tf_op jit(solution)/shard_map/ppermute | solution.py:202
  34.9 5.6 %collective-permute-start.10 = (bf16[2,128,128]{2,1,0:T(8,128)(2,1)S(1)}, bf16[2,128,128]{2,1,0:T(8,128)(2,1)S(1)}, u32[]{:S(2)}, u32[]{:S(2)}) collective-permute-start(bf16[2,128,128]{2,1,0:T(8,128)(2,1)S(1)} %get-tuple-element.35), channel_id=1, source_target_pairs={{0,6},{2,4},{4,2},{6,0},{8,14},{10,12},{12,10},{14,8},{1,7},{3,5},... | collective-permute-start | bytes 196616 | tf_op jit(solution)/shard_map/ppermute | solution.py:202
  35.5 5.3 %collective-permute-start.11 = (bf16[2,128,128]{2,1,0:T(8,128)(2,1)S(1)}, bf16[2,128,128]{2,1,0:T(8,128)(2,1)S(1)}, u32[]{:S(2)}, u32[]{:S(2)}) collective-permute-start(bf16[2,128,128]{2,1,0:T(8,128)(2,1)S(1)} %get-tuple-element.34), channel_id=1, source_target_pairs={{0,2},{2,0},{4,6},{6,4},{8,10},{10,8},{12,14},{14,12},{1,3},{3,1},... | collective-permute-start | bytes 196616 | tf_op jit(solution)/shard_map/ppermute | solution.py:202
  36.7 4.7 %collective-permute-start.9 = (bf16[2,128,128]{2,1,0:T(8,128)(2,1)S(1)}, bf16[2,128,128]{2,1,0:T(8,128)(2,1)S(1)}, u32[]{:S(2)}, u32[]{:S(2)}) collective-permute-start(bf16[2,128,128]{2,1,0:T(8,128)(2,1)S(1)} %get-tuple-element.33), channel_id=1, source_target_pairs={{0,4},{2,6},{4,0},{6,2},{8,12},{10,14},{12,8},{14,10},{1,5},{3,7},... | collective-permute-start | bytes 196616 | tf_op jit(solution)/shard_map/ppermute | solution.py:202
  41.4 4.9 %collective-permute-start.12 = (bf16[128,128]{1,0:T(8,128)(2,1)S(1)}, bf16[128,128]{1,0:T(8,128)(2,1)S(1)}, u32[]{:S(2)}, u32[]{:S(2)}) collective-permute-start(bf16[128,128]{1,0:T(8,128)(2,1)S(1)} %fusion.4), channel_id=1, source_target_pairs={{0,8},{2,10},{4,12},{6,14},{8,0},{10,2},{12,4},{14,6},{1,9},{3,11}... | collective-permute-start | bytes 98312 | tf_op jit(solution)/shard_map/ppermute | solution.py:202

commit v6 on v5

--- a/solution.py
+++ b/solution.py
@@ -33,8 +33,16 @@
     return high, (a - high.astype(F32)).astype(BF16)
 
 
-def pack_kernel(peers, feats, *ordered):
+def pack_kernel(peers, hbm, *refs):
+    *ordered, feats, sems = refs
     outs = dict(zip(ORDER, ordered))
+    half = feats.shape[0] // 2
+    copies = [
+        pltpu.make_async_copy(hbm.at[pl.ds(i * half, half)], feats.at[pl.ds(i * half, half)], sems.at[i])
+        for i in range(2)
+    ]
+    for copy in copies:
+        copy.start()
     ex_dev, modules, feat = feats.shape
     cols = feat // LANES
     step = 256 // modules
@@ -47,6 +55,8 @@
 
     acc = jnp.zeros((8, feat), F32)
     for b in range(ex_dev // step):
+        if b * step % half == 0:
+            copies[b * step // half].wait()
         x = feats[b * step : (b + 1) * step].reshape(step * modules, feat)
         y = dot(pick, x, ((1,), (0,))).astype(BF16)
         for k in range(peers):
@@ -73,11 +83,12 @@
     outs = pl.pallas_call(
         functools.partial(pack_kernel, peers),
         out_shape=[shape] * peers,
-        in_specs=[VMEM],
+        in_specs=[pl.BlockSpec(memory_space=pltpu.HBM)],
         out_specs=[VMEM] * peers,
+        scratch_shapes=[pltpu.VMEM(features.shape, BF16), pltpu.SemaphoreType.DMA((2,))],
         compiler_params=limit(8),
         name="pack",
-    )(features)
+    )(pltpu.with_memory_space_constraint(features, pltpu.HBM))
     return dict(zip(ORDER, outs))
 
 

time: 47.1 us -> 47.1 us (level)
  local copies, waits for them, and re-layouts: 1.62 us -> 0.03 us
  Pallas kernels: 5.16 us -> 6.72 us
    unnamed x6 -> x4, local copies, waits for them, and re-layouts: 1.6 us -> 0.01 us
    pallas_call x1, Pallas kernels: 0.45 us -> 2.02 us  [pack(): pl.pallas_call(functools.partial(pack_kernel, peers), out_shape=[shape] *...]
where the time goes in v6:
time: 47.1 us; the launch traced here: 46.9 us
  starting transfers between devices  24.8 us (53%)
  waiting for transfers between devices  14.5 us (31%)
  Pallas kernels  6.72 us (14%)
  other arithmetic  0.76 us (2%)
    ppermute x13, starting transfers between devices, exchange(): return lax.ppermute(x, axes, [(i, i ^ k) for i in range(size)])  24.8 us
    ppermute x13, waiting for transfers between devices, exchange(): return lax.ppermute(x, axes, [(i, i ^ k) for i in range(size)])  14.5 us
    pallas_call x1, Pallas kernels, score(): pl.pallas_call(functools.partial(score_kernel, modules), out_shape=[jax.S...  3.29 us
    pallas_call x1, Pallas kernels, pack(): pl.pallas_call(functools.partial(pack_kernel, peers), out_shape=[shape] *...  2.02 us
  transfers between devices with their start and end apart: 13, of which 7 were waited for; matrix products, arithmetic and copies ran while one was open for 0% of the time, Pallas kernels for 3%

profile of v6, /device:TPU:0, one launch (start us, length us, event | category | flops | bytes accessed | tf_op | source)
XLA Modules:
  0.0 46.9 jit_solution(16282938091870215762)
XLA Ops:
  0.0 0.0 copy-start.1
  0.0 0.0 copy-start
  0.0 2.0 %pack.1 = (bf16[520,128]{1,0:T(8,128)(2,1)S(1)}, bf16[520,128]{1,0:T(8,128)(2,1)S(1)}, bf16[520,128]{1,0:T(8,128)(2,1)S(1)}, bf16[520,128]{1,0:T(8,128)(2,1)S(1)...) custom-call(bf16[128,16,512]{2,1,0:T(8,128)(2,1)} %hbm.1), custom_call_target="tpu_custom_call" | custom-call | tf_op jit(solution)/shard_map/pack/pallas_call | solution.py:83
  2.0 5.1 %collective-permute-start.2 = (bf16[520,128]{1,0:T(8,128)(2,1)S(1)}, bf16[520,128]{1,0:T(8,128)(2,1)S(1)}, u32[]{:S(2)}, u32[]{:S(2)}) collective-permute-start(bf16[520,128]{1,0:T(8,128)(2,1)S(1)} %get-tuple-element.20), channel_id=1, source_target_pairs={{0,12},{2,14},{4,8},{6,10},{8,4},{10,6},{12,0},{14,2},{1,13},{3,15... | collective-permute-start | bytes 399368 | tf_op jit(solution)/shard_map/ppermute | solution.py:213
  7.1 0.4 collective-permute-start.3
  7.5 0.0 copy-done.1
  7.5 0.0 collective-permute-start.7
  7.5 2.4 %collective-permute-start.4 = (bf16[520,128]{1,0:T(8,128)(2,1)S(1)}, bf16[520,128]{1,0:T(8,128)(2,1)S(1)}, u32[]{:S(2)}, u32[]{:S(2)}) collective-permute-start(bf16[520,128]{1,0:T(8,128)(2,1)S(1)} %get-tuple-element.22), channel_id=1, source_target_pairs={{0,14},{2,12},{4,10},{6,8},{8,6},{10,4},{12,2},{14,0},{1,15},{3,13... | collective-permute-start | bytes 399368 | tf_op jit(solution)/shard_map/ppermute | solution.py:213
  10.0 2.5 %collective-permute-start.5 = (bf16[520,128]{1,0:T(8,128)(2,1)S(1)}, bf16[520,128]{1,0:T(8,128)(2,1)S(1)}, u32[]{:S(2)}, u32[]{:S(2)}) collective-permute-start(bf16[520,128]{1,0:T(8,128)(2,1)S(1)} %get-tuple-element.23), channel_id=1, source_target_pairs={{0,6},{2,4},{4,2},{6,0},{8,14},{10,12},{12,10},{14,8},{1,7},{3,5},... | collective-permute-start | bytes 399368 | tf_op jit(solution)/shard_map/ppermute | solution.py:213
  12.5 0.0 collective-permute-done.7
  12.5 0.5 collective-permute-start.6
  12.9 0.0 collective-permute-done.2.refs_0_
  12.9 7.9 %collective-permute-start = (bf16[520,128]{1,0:T(8,128)(2,1)S(1)}, bf16[520,128]{1,0:T(8,128)(2,1)S(1)}, u32[]{:S(2)}, u32[]{:S(2)}) collective-permute-start(bf16[520,128]{1,0:T(8,128)(2,1)S(1)} %get-tuple-element.18), channel_id=1, source_target_pairs={{0,8},{2,10},{4,12},{6,14},{8,0},{10,2},{12,4},{14,6},{1,9},{3,11}... | collective-permute-start | bytes 399368 | tf_op jit(solution)/shard_map/ppermute | solution.py:213
  20.8 3.4 %collective-permute-done.3.refs_1_ = bf16[520,128]{1,0:T(8,128)(2,1)S(1)} collective-permute-done((bf16[520,128]{1,0:T(8,128)(2,1)S(1)}, bf16[520,128]{1,0:T(8,128)(2,1)S(1)}, u32[]{:S(2)}, u32[]{:S(2)}) %collective-permute-start.3) | collective-permute-done | bytes 133152 | tf_op jit(solution)/shard_map/ppermute | solution.py:213
  24.2 0.0 collective-permute-start.1
  24.2 0.0 copy-done
  24.2 0.8 %pick.1.refs_5_ = bf16[256,512]{1,0:T(8,128)(2,1)S(1)} custom-call(bf16[512,4,512]{2,1,0:T(4,128)(2,1)S(1)} %copy-done, s32[1,256]{1,0:T(1,128)S(1)} %bitcast.21), custom_call_target="tpu_custom_call" | custom-call | tf_op jit(solution)/shard_map/pick/pallas_call | solution.py:106
  25.0 0.0 collective-permute-done.4.refs_2_
  25.0 0.0 collective-permute-done.5.refs_3_
  25.0 0.0 collective-permute-done.6.refs_4_
  25.0 0.7 %early.1 = (bf16[768,512]{1,0:T(8,128)(2,1)S(1)}, f32[512,512]{1,0:T(8,128)S(1)}, f32[8,128]{1,0:T(8,128)S(1)}) custom-call(bf16[520,128]{1,0:T(8,128)(2,1)S(1)} %collective-permute-done.2.refs_0_, bf16[520,128]{1,0:T(8,128)(2,1)S(1)} %collective-permute-done.3.refs_1_, bf16[520,128]{1,0:T(8,128)(2,1)S(1)} %collective-permute-done.4.refs_2_, ...), custom_call_target="tpu_custom_call" | custom-call | flops 402653184 | bytes 4194304 | tf_op jit(solution)/shard_map/early/pallas_call | solution.py:140
  25.7 4.1 %collective-permute-done.refs_0_ = bf16[520,128]{1,0:T(8,128)(2,1)S(1)} collective-permute-done((bf16[520,128]{1,0:T(8,128)(2,1)S(1)}, bf16[520,128]{1,0:T(8,128)(2,1)S(1)}, u32[]{:S(2)}, u32[]{:S(2)}) %collective-permute-start) | collective-permute-done | bytes 133152 | tf_op jit(solution)/shard_map/ppermute | solution.py:213
  29.8 0.0 collective-permute-done.1.refs_1_
  29.8 3.3 %score.1 = (f32[4,2,128,128]{3,2,1,0:T(8,128)S(1)}, bf16[4,2,128,128]{3,2,1,0:T(8,128)(2,1)S(1)}) custom-call(bf16[520,128]{1,0:T(8,128)(2,1)S(1)} %collective-permute-done.refs_0_, bf16[520,128]{1,0:T(8,128)(2,1)S(1)} %collective-permute-done.1.refs_1_, bf16[768,512]{1,0:T(8,128)(2,1)S(1)} %get-tuple-element.26.refs_2_, ...), custom_call_target="tpu_custom_call" | custom-call | tf_op jit(solution)/shard_map/score/pallas_call | solution.py:201
  33.1 0.1 collective-permute-start.8
  33.2 1.5 %collective-permute-done.8 = bf16[4,2,128,128]{3,2,1,0:T(8,128)(2,1)S(1)} collective-permute-done((bf16[4,2,128,128]{3,2,1,0:T(8,128)(2,1)S(1)}, bf16[4,2,128,128]{3,2,1,0:T(8,128)(2,1)S(1)}, u32[]{:S(2)}, u32[]{:S(2)}) %collective-permute-start.8) | collective-permute-done | bytes 262176 | tf_op jit(solution)/shard_map/ppermute | solution.py:213
  34.7 0.1 fusion.5
  34.8 0.6 %collective-permute-start.10 = (bf16[2,128,128]{2,1,0:T(8,128)(2,1)S(1)}, bf16[2,128,128]{2,1,0:T(8,128)(2,1)S(1)}, u32[]{:S(2)}, u32[]{:S(2)}) collective-permute-start(bf16[2,128,128]{2,1,0:T(8,128)(2,1)S(1)} %get-tuple-element.35), channel_id=1, source_target_pairs={{0,6},{2,4},{4,2},{6,0},{8,14},{10,12},{12,10},{14,8},{1,7},{3,5},... | collective-permute-start | bytes 196616 | tf_op jit(solution)/shard_map/ppermute | solution.py:213
  35.5 1.2 %collective-permute-start.11 = (bf16[2,128,128]{2,1,0:T(8,128)(2,1)S(1)}, bf16[2,128,128]{2,1,0:T(8,128)(2,1)S(1)}, u32[]{:S(2)}, u32[]{:S(2)}) collective-permute-start(bf16[2,128,128]{2,1,0:T(8,128)(2,1)S(1)} %get-tuple-element.34), channel_id=1, source_target_pairs={{0,2},{2,0},{4,6},{6,4},{8,10},{10,8},{12,14},{14,12},{1,3},{3,1},... | collective-permute-start | bytes 196616 | tf_op jit(solution)/shard_map/ppermute | solution.py:213
  36.6 1.7 %collective-permute-start.9 = (bf16[2,128,128]{2,1,0:T(8,128)(2,1)S(1)}, bf16[2,128,128]{2,1,0:T(8,128)(2,1)S(1)}, u32[]{:S(2)}, u32[]{:S(2)}) collective-permute-start(bf16[2,128,128]{2,1,0:T(8,128)(2,1)S(1)} %get-tuple-element.33), channel_id=1, source_target_pairs={{0,4},{2,6},{4,0},{6,2},{8,12},{10,14},{12,8},{14,10},{1,5},{3,7},... | collective-permute-start | bytes 196616 | tf_op jit(solution)/shard_map/ppermute | solution.py:213
  38.4 2.1 %collective-permute-done.10 = bf16[2,128,128]{2,1,0:T(8,128)(2,1)S(1)} collective-permute-done((bf16[2,128,128]{2,1,0:T(8,128)(2,1)S(1)}, bf16[2,128,128]{2,1,0:T(8,128)(2,1)S(1)}, u32[]{:S(2)}, u32[]{:S(2)}) %collective-permute-start.10) | collective-permute-done | bytes 65568 | tf_op jit(solution)/shard_map/ppermute | solution.py:213
  40.5 0.3 collective-permute-done.11
  40.7 0.6 %collective-permute-done.9 = bf16[2,128,128]{2,1,0:T(8,128)(2,1)S(1)} collective-permute-done((bf16[2,128,128]{2,1,0:T(8,128)(2,1)S(1)}, bf16[2,128,128]{2,1,0:T(8,128)(2,1)S(1)}, u32[]{:S(2)}, u32[]{:S(2)}) %collective-permute-start.9) | collective-permute-done | bytes 65568 | tf_op jit(solution)/shard_map/ppermute | solution.py:213
  41.4 2.4 %collective-permute-start.12 = (bf16[128,128]{1,0:T(8,128)(2,1)S(1)}, bf16[128,128]{1,0:T(8,128)(2,1)S(1)}, u32[]{:S(2)}, u32[]{:S(2)}) collective-permute-start(bf16[128,128]{1,0:T(8,128)(2,1)S(1)} %fusion.4), channel_id=1, source_target_pairs={{0,8},{2,10},{4,12},{6,14},{8,0},{10,2},{12,4},{14,6},{1,9},{3,11}... | collective-permute-start | bytes 98312 | tf_op jit(solution)/shard_map/ppermute | solution.py:213
  43.8 2.5 %collective-permute-done.12 = bf16[128,128]{1,0:T(8,128)(2,1)S(1)} collective-permute-done((bf16[128,128]{1,0:T(8,128)(2,1)S(1)}, bf16[128,128]{1,0:T(8,128)(2,1)S(1)}, u32[]{:S(2)}, u32[]{:S(2)}) %collective-permute-start.12) | collective-permute-done | bytes 32800 | tf_op jit(solution)/shard_map/ppermute | solution.py:213
  46.3 0.6 %fusion.3 = f32[128,128]{1,0:T(8,128)} fusion(f32[2,128,128]{2,1,0:T(8,128)S(1)} %fusion.2, bf16[128,128]{1,0:T(8,128)(2,1)S(1)} %collective-permute-done.12), kind=kLoop, calls=%fused_computation.7 | loop fusion | flops 32768 | bytes 163840 | tf_op jit(solution)/shard_map/add | solution.py:230
  (4 shorter events, 0.1 us)
Async XLA Ops:
  0.0 7.5 %copy-start.1 = (s32[128]{0:T(128)S(1)}, s32[128]{0:T(128)}, u32[]{:S(2)}) copy-start(s32[128]{0:T(128)} %param.5) | copy-start | bytes 1540
  0.0 24.2 %copy-start = (bf16[512,4,512]{2,1,0:T(4,128)(2,1)S(1)}, bf16[512,4,512]{2,1,0:T(4,128)(2,1)}, u32[]{:S(2)}) copy-start(bf16[512,4,512]{2,1,0:T(4,128)(2,1)} %pool.1) | copy-start | bytes 6291460
  2.0 10.9 %collective-permute-start.2 = (bf16[520,128]{1,0:T(8,128)(2,1)S(1)}, bf16[520,128]{1,0:T(8,128)(2,1)S(1)}, u32[]{:S(2)}, u32[]{:S(2)}) collective-permute-start(bf16[520,128]{1,0:T(8,128)(2,1)S(1)} %get-tuple-element.20), channel_id=1, source_target_pairs={{0,12},{2,14},{4,8},{6,10},{8,4},{10,6},{12,0},{14,2},{1,13},{3,15... | collective-permute-start | bytes 399368 | tf_op jit(solution)/shard_map/ppermute | solution.py:213
  7.1 17.0 %collective-permute-start.3 = (bf16[520,128]{1,0:T(8,128)(2,1)S(1)}, bf16[520,128]{1,0:T(8,128)(2,1)S(1)}, u32[]{:S(2)}, u32[]{:S(2)}) collective-permute-start(bf16[520,128]{1,0:T(8,128)(2,1)S(1)} %get-tuple-element.21), channel_id=1, source_target_pairs={{0,10},{2,8},{4,14},{6,12},{8,2},{10,0},{12,6},{14,4},{1,11},{3,9}... | collective-permute-start | bytes 399368 | tf_op jit(solution)/shard_map/ppermute | solution.py:213
  7.5 5.0 %collective-permute-start.7 = (s32[128]{0:T(128)S(1)}, s32[128]{0:T(128)S(1)}, u32[]{:S(2)}, u32[]{:S(2)}) collective-permute-start(s32[128]{0:T(128)S(1)} %copy-done.1), channel_id=1, source_target_pairs={{0,1},{1,0},{2,3},{3,2},{4,5},{5,4},{6,7},{7,6},{8,9},{9,8},{10,11... | collective-permute-start | bytes 1544 | tf_op jit(solution)/shard_map/ppermute | solution.py:213
  7.5 17.5 %collective-permute-start.4 = (bf16[520,128]{1,0:T(8,128)(2,1)S(1)}, bf16[520,128]{1,0:T(8,128)(2,1)S(1)}, u32[]{:S(2)}, u32[]{:S(2)}) collective-permute-start(bf16[520,128]{1,0:T(8,128)(2,1)S(1)} %get-tuple-element.22), channel_id=1, source_target_pairs={{0,14},{2,12},{4,10},{6,8},{8,6},{10,4},{12,2},{14,0},{1,15},{3,13... | collective-permute-start | bytes 399368 | tf_op jit(solution)/shard_map/ppermute | solution.py:213
  10.0 15.1 %collective-permute-start.5 = (bf16[520,128]{1,0:T(8,128)(2,1)S(1)}, bf16[520,128]{1,0:T(8,128)(2,1)S(1)}, u32[]{:S(2)}, u32[]{:S(2)}) collective-permute-start(bf16[520,128]{1,0:T(8,128)(2,1)S(1)} %get-tuple-element.23), channel_id=1, source_target_pairs={{0,6},{2,4},{4,2},{6,0},{8,14},{10,12},{12,10},{14,8},{1,7},{3,5},... | collective-permute-start | bytes 399368 | tf_op jit(solution)/shard_map/ppermute | solution.py:213
  12.5 12.6 %collective-permute-start.6 = (bf16[520,128]{1,0:T(8,128)(2,1)S(1)}, bf16[520,128]{1,0:T(8,128)(2,1)S(1)}, u32[]{:S(2)}, u32[]{:S(2)}) collective-permute-start(bf16[520,128]{1,0:T(8,128)(2,1)S(1)} %get-tuple-element.24), channel_id=1, source_target_pairs={{0,4},{2,6},{4,0},{6,2},{8,12},{10,14},{12,8},{14,10},{1,5},{3,7},... | collective-permute-start | bytes 399368 | tf_op jit(solution)/shard_map/ppermute | solution.py:213
  12.9 16.9 %collective-permute-start = (bf16[520,128]{1,0:T(8,128)(2,1)S(1)}, bf16[520,128]{1,0:T(8,128)(2,1)S(1)}, u32[]{:S(2)}, u32[]{:S(2)}) collective-permute-start(bf16[520,128]{1,0:T(8,128)(2,1)S(1)} %get-tuple-element.18), channel_id=1, source_target_pairs={{0,8},{2,10},{4,12},{6,14},{8,0},{10,2},{12,4},{14,6},{1,9},{3,11}... | collective-permute-start | bytes 399368 | tf_op jit(solution)/shard_map/ppermute | solution.py:213
  24.2 5.6 %collective-permute-start.1 = (bf16[520,128]{1,0:T(8,128)(2,1)S(1)}, bf16[520,128]{1,0:T(8,128)(2,1)S(1)}, u32[]{:S(2)}, u32[]{:S(2)}) collective-permute-start(bf16[520,128]{1,0:T(8,128)(2,1)S(1)} %get-tuple-element.19), channel_id=1, source_target_pairs={{0,2},{2,0},{4,6},{6,4},{8,10},{10,8},{12,14},{14,12},{1,3},{3,1},... | collective-permute-start | bytes 399368 | tf_op jit(solution)/shard_map/ppermute | solution.py:213
  33.1 1.6 %collective-permute-start.8 = (bf16[4,2,128,128]{3,2,1,0:T(8,128)(2,1)S(1)}, bf16[4,2,128,128]{3,2,1,0:T(8,128)(2,1)S(1)}, u32[]{:S(2)}, u32[]{:S(2)}) collective-permute-start(bf16[4,2,128,128]{3,2,1,0:T(8,128)(2,1)S(1)} %get-tuple-element.30), channel_id=1, source_target_pairs={{0,1},{1,0},{2,3},{3,2},{4,5},{5,4},{6,7},{7,6},{8,9},{9,8},{10,11... | collective-permute-start | bytes 786440 | tf_op jit(solution)/shard_map/ppermute | solution.py:213
  34.8 5.6 %collective-permute-start.10 = (bf16[2,128,128]{2,1,0:T(8,128)(2,1)S(1)}, bf16[2,128,128]{2,1,0:T(8,128)(2,1)S(1)}, u32[]{:S(2)}, u32[]{:S(2)}) collective-permute-start(bf16[2,128,128]{2,1,0:T(8,128)(2,1)S(1)} %get-tuple-element.35), channel_id=1, source_target_pairs={{0,6},{2,4},{4,2},{6,0},{8,14},{10,12},{12,10},{14,8},{1,7},{3,5},... | collective-permute-start | bytes 196616 | tf_op jit(solution)/shard_map/ppermute | solution.py:213
  35.5 5.3 %collective-permute-start.11 = (bf16[2,128,128]{2,1,0:T(8,128)(2,1)S(1)}, bf16[2,128,128]{2,1,0:T(8,128)(2,1)S(1)}, u32[]{:S(2)}, u32[]{:S(2)}) collective-permute-start(bf16[2,128,128]{2,1,0:T(8,128)(2,1)S(1)} %get-tuple-element.34), channel_id=1, source_target_pairs={{0,2},{2,0},{4,6},{6,4},{8,10},{10,8},{12,14},{14,12},{1,3},{3,1},... | collective-permute-start | bytes 196616 | tf_op jit(solution)/shard_map/ppermute | solution.py:213
  36.6 4.7 %collective-permute-start.9 = (bf16[2,128,128]{2,1,0:T(8,128)(2,1)S(1)}, bf16[2,128,128]{2,1,0:T(8,128)(2,1)S(1)}, u32[]{:S(2)}, u32[]{:S(2)}) collective-permute-start(bf16[2,128,128]{2,1,0:T(8,128)(2,1)S(1)} %get-tuple-element.33), channel_id=1, source_target_pairs={{0,4},{2,6},{4,0},{6,2},{8,12},{10,14},{12,8},{14,10},{1,5},{3,7},... | collective-permute-start | bytes 196616 | tf_op jit(solution)/shard_map/ppermute | solution.py:213
  41.4 4.9 %collective-permute-start.12 = (bf16[128,128]{1,0:T(8,128)(2,1)S(1)}, bf16[128,128]{1,0:T(8,128)(2,1)S(1)}, u32[]{:S(2)}, u32[]{:S(2)}) collective-permute-start(bf16[128,128]{1,0:T(8,128)(2,1)S(1)} %fusion.4), channel_id=1, source_target_pairs={{0,8},{2,10},{4,12},{6,14},{8,0},{10,2},{12,4},{14,6},{1,9},{3,11}... | collective-permute-start | bytes 98312 | tf_op jit(solution)/shard_map/ppermute | solution.py:213
